TPU v7x, 128 devices: a whole 4x4x4 slice. The times are simulated.
128 devices in a mesh: gx: 8 (over x, core), gy: 16 (over y, z).
Axes of the slice: x: 4, y: 4, z: 4, core: 2. Of those that a mesh axis runs over, the one named last changes fastest.
Arguments:
- emission: bfloat16 [393216, 128], P(('gx', 'gy')), may hold values from -6 to 6
- reflectance: float32 [393216], P(('gx', 'gy')), may hold values from 0.3 to 0.9
- link_blocks: bfloat16 [18432, 256, 256], P(('gx', 'gy')), may hold values from -0.109375 to 0.109375
- link_source: int32 [18432], P(('gx', 'gy')), may hold values from 0 to 11
- link_target: int32 [18432, 1], P(('gx', 'gy')), may hold values from 0 to 127, as said below
- link_slot: int32 [18432], P(('gx', 'gy')), may hold values from 0 to 11
- sensor_cell: int32 [65536, 8], P(('gx', 'gy')), may hold values from 0 to 9215
- sensor_weight: float32 [65536, 8], P(('gx', 'gy')), may hold values from 0 to 0.25
Outputs:
- radiosity: float32 [393216, 128], P(('gx', 'gy'))
- sensor_values: float32 [65536, 128], P(('gx', 'gy'))
Inputs may be any that keep to these rules, and one draw needn't show every extreme that they name: `link_target`: the owner of each block is the device that holds it or one of that device's neighbours (i +- 1, j) or (i, j +- 1) inside the grid of devices, without wrapping. Among the 144 blocks of one device at most 9 name any one neighbour, and some neighbour is named exactly 9 times.
All inputs are finite; a program needn't handle non-finite values.
Results may differ from a plain program's by a relative error of at most 0.0039.
Values may be sent and summed in bfloat16 or wider, within the bound.
No kernel may reach another device: no remote copies, remote signals or barrier semaphores. Data moves between devices by JAX's collectives and lax.ppermute only.
A program may use at most 128 MiB of HBM per device.

v0:
```python
import functools

import jax
import jax.numpy as jnp
from jax import lax
from jax.experimental import pallas as pl
from jax.experimental.pallas import tpu as pltpu
from jax.sharding import PartitionSpec as P

BF16, F32, I32, I16 = jnp.bfloat16, jnp.float32, jnp.int32, jnp.int16
P_SIZE = 256
S = 128
CL = 12
SENS = 512
TAPS = 8
LINKS = 144
CAP = 9
ROWS = CL * P_SIZE
TERM_ROWS = CAP * P_SIZE
SLOT_ROWS = 16
META_ROWS = 3 * TAPS * SENS // S
GX_ROWS = TERM_ROWS + SLOT_ROWS
GY_ROWS = GX_ROWS + META_ROWS
OWN_PAD = LINKS + 16
GROUP = 16
MIB = 1 << 20

VM = pl.BlockSpec(memory_space=pltpu.VMEM)
SM = pl.BlockSpec(memory_space=pltpu.SMEM)
ANY = pl.BlockSpec(memory_space=pl.ANY)

PAIR = 2 * CAP
SPARE = 3 * PAIR
OWN_SRC, OWN_AIM, OWN_COUNT = OWN_PAD, 2 * OWN_PAD, 3 * OWN_PAD
CHUNK = 16


def params(mib):
    return pltpu.CompilerParams(vmem_limit_bytes=mib * MIB)


def on_chip(x):
    return pltpu.with_memory_space_constraint(x, pltpu.VMEM)


def partners(n_cols):
    i, j = lax.axis_index("gx"), lax.axis_index("gy")
    here = i * n_cols + j
    step_y, step_x = 1 - 2 * (j % 2), 1 - 2 * (i % 2)
    return here, (
        here + step_y,
        here - step_y,
        here + step_x * n_cols,
        here - step_x * n_cols,
    )


def dot(a, b):
    return jnp.dot(a, b, preferred_element_type=F32)


def in_hbm(x):
    return pltpu.with_memory_space_constraint(x, pltpu.HBM)


def settle(tab, counts, source, slot):
    for p in range(PAIR):
        filled = p % CAP < counts[p // CAP]
        link = jnp.where(filled, tab[p], 0)
        tab[p] = link
        tab[PAIR + p] = source[link]
        tab[2 * PAIR + p] = jnp.where(filled, slot[link] + 1, 0)


def fetch(tab, blocks, buf, sems):
    copies = [pltpu.make_async_copy(blocks.at[tab[p]], buf.at[p], sems.at[p]) for p in range(PAIR)]
    for copy in copies:
        copy.start()
    return copies


def send_terms(tab, block, field, packs):
    for p in range(PAIR):
        term = jnp.where(tab[2 * PAIR + p] > 0, dot(block(p), field[tab[PAIR + p]]), 0.0)
        packs[p // CAP][pl.ds((p % CAP) * P_SIZE, P_SIZE), :] = term.astype(BF16)


def put_slots(tab, packs):
    row = lax.broadcasted_iota(I32, (SLOT_ROWS, S), 0)
    for side in range(2):
        slots = jnp.zeros((SLOT_ROWS, S), I32)
        for k in range(CAP):
            slots = jnp.where(row == k, tab[2 * PAIR + side * CAP + k], slots)
        packs[side][pl.ds(TERM_ROWS, SLOT_ROWS), :] = slots.astype(F32).astype(BF16)


def sensor_rows(cells, weights, weights_sum, packs):
    cell, weight = cells[...], weights[...]
    total = weight
    for shift in range(1, TAPS):
        same = pltpu.roll(cell, shift, 0) == cell
        total = total + jnp.where(same, pltpu.roll(weight, shift, 0), 0.0)
    weights_sum[...] = total
    meta = []
    for part in ((cell >> 7).astype(F32), (cell & 127).astype(F32), total):
        for q in range(SENS // S):
            meta.append(part[:, q * S : (q + 1) * S])
    meta = jnp.concatenate(meta, axis=0).astype(BF16)
    for pack in packs:
        pack[pl.ds(GX_ROWS, META_ROWS), :] = meta


def first_kernel(
    n_cols, target, source, slot, emission, blocks, cells, weights,
    pack_e, pack_o, tab, weights_sum, field, buf, sems, sem_field,
):
    field_copy = pltpu.make_async_copy(emission, field, sem_field)
    field_copy.start()
    gy_e, gy_o, _, _ = partners(n_cols)[1]

    def scan(link, counts):
        owner = target[0, link]
        even, odd = owner == gy_e, owner == gy_o
        tab[jnp.where(even, counts[0], jnp.where(odd, CAP + counts[1], SPARE))] = link
        return counts[0] + even.astype(I32), counts[1] + odd.astype(I32)

    counts = lax.fori_loop(0, LINKS, scan, (jnp.int32(0),) * 2, unroll=8)
    settle(tab, counts, source, slot)
    copies = fetch(tab, blocks, buf, sems)
    packs = (pack_e, pack_o)
    put_slots(tab, packs)
    sensor_rows(cells, weights, weights_sum, packs)
    field_copy.wait()
    for copy in copies:
        copy.wait()
    send_terms(tab, lambda p: buf[p], field, packs)


def gx_kernel(
    n_cols, target, source, slot, emission, blocks,
    pack_e, pack_o, tab, own, field, buf, sems, sem_field,
):
    field_copy = pltpu.make_async_copy(emission, field, sem_field)
    field_copy.start()
    gy_e, gy_o, gx_e, gx_o = partners(n_cols)[1]

    def scan(link, counts):
        owner = target[0, link]
        even, odd = owner == gx_e, owner == gx_o
        other = even | odd | (owner == gy_e) | (owner == gy_o)
        tab[jnp.where(even, counts[0], jnp.where(odd, CAP + counts[1], SPARE))] = link
        own[counts[2]] = link
        return (
            counts[0] + even.astype(I32),
            counts[1] + odd.astype(I32),
            counts[2] + jnp.where(other, 0, 1),
        )

    counts = lax.fori_loop(0, LINKS, scan, (jnp.int32(0),) * 3, unroll=8)
    settle(tab, counts, source, slot)
    copies = fetch(tab, blocks, buf, sems)
    packs = (pack_e, pack_o)
    put_slots(tab, packs)
    field_copy.wait()
    for copy in copies:
        copy.wait()
    send_terms(tab, lambda p: buf[p], field, packs)
    for k in range(GROUP):
        own[counts[2] + k] = 0
    groups = (counts[2] + GROUP - 1) // GROUP
    own[OWN_COUNT] = groups

    def look_up(n, _):
        link = own[n]
        own[OWN_SRC + n] = source[link]
        own[OWN_AIM + n] = jnp.where(n < counts[2], slot[link], CL)
        return 0

    def look_up_group(g, _):
        for u in range(GROUP):
            look_up(g * GROUP + u, 0)
        return 0

    lax.fori_loop(0, groups, look_up_group, 0)


def own_terms(own, blocks, field, acc, before_group):
    acc[...] = jnp.zeros_like(acc)

    def group(g, state):
        state = before_group(g, state)
        terms = []
        for u in range(GROUP):
            n = g * GROUP + u
            terms.append(dot(blocks[own[n]], field[own[OWN_SRC + n]]).astype(BF16))
        for u in range(GROUP):
            acc[own[OWN_AIM + g * GROUP + u]] += terms[u].astype(F32)
        return state

    return lax.fori_loop(0, own[OWN_COUNT], group, jnp.int32(0))


def own_first_kernel(own, blocks_far, emission, rho, acc, rho_full, blocks, field, sems, sem_field):
    field_copy = pltpu.make_async_copy(emission, field, sem_field)
    field_copy.start()
    chunks = LINKS // CHUNK

    def copy(c):
        part = pl.ds(c * CHUNK, CHUNK)
        return pltpu.make_async_copy(blocks_far.at[part], blocks.at[part], sems.at[c])

    for c in range(chunks):
        copy(c).start()
    for q in range(ROWS // S):
        wide = jnp.broadcast_to(rho[pl.ds(q, 1), :], (S, S))
        rho_full[pl.ds(q * S, S), :] = wide.T
    field_copy.wait()

    def take(c, _):
        copy(c).wait()
        return 0

    def before_group(g, waited):
        last = jnp.where(g + 1 == own[OWN_COUNT], LINKS - 1, own[g * GROUP + GROUP - 1])
        needed = jnp.maximum(waited, (last >> 4) + 1)
        lax.fori_loop(waited, needed, take, 0)
        return needed

    waited = own_terms(own, blocks, field, acc, before_group)
    lax.fori_loop(waited, chunks, take, 0)


def own_kernel(own, blocks, field, acc):
    own_terms(own, blocks, field, acc, lambda g, state: state)


def slots_of(arrived):
    out = []
    for ref in arrived:
        values = ref[pl.ds(TERM_ROWS, SLOT_ROWS), :].astype(F32).astype(I32)
        for k in range(CAP):
            value = values[k, 0]
            out.append(jnp.where(value == 0, CL, value - 1))
    return out


def add_arrived(aims, arrived, acc):
    for n, aim in enumerate(aims):
        rows = pl.ds((n % CAP) * P_SIZE, P_SIZE)
        acc[aim] += arrived[n // CAP][rows, :].astype(F32)


def radiosity_of(emission, rho_full, acc, c):
    rows = pl.ds(c * P_SIZE, P_SIZE)
    return emission[rows, :].astype(F32) + rho_full[rows, :] * acc[c]


def second_kernel(
    tab_y, tab_x, blocks, emission, rho_full, acc_in, gy_e, gy_o, gx_e, gx_o,
    out_gy_e, out_gy_o, out_gx_e, out_gx_o, field, aims_out, acc, base, sem_base,
):
    del acc_in
    base_copy = pltpu.make_async_copy(emission, base, sem_base)
    base_copy.start()
    arrived = (gy_e, gy_o, gx_e, gx_o)
    aims = slots_of(arrived)
    for n, aim in enumerate(aims):
        aims_out[n] = aim
    add_arrived(aims, arrived, acc)
    base_copy.wait()
    for c in range(CL):
        field[c] = radiosity_of(base, rho_full, acc, c).astype(BF16)
    send_terms(tab_y, lambda p: blocks[tab_y[p]], field, (out_gy_e, out_gy_o))
    send_terms(tab_x, lambda p: blocks[tab_x[p]], field, (out_gx_e, out_gx_o))


def spread(cell_rows, weight_rows, out):
    tile, steps = 16, 8
    for q in range(SENS // S):
        cells = [jnp.broadcast_to(cell_rows(k, q), (tile, S)).astype(I16) for k in range(TAPS)]
        weights = [jnp.broadcast_to(weight_rows(k, q), (tile, S)).astype(BF16) for k in range(TAPS)]

        def fill(n, first):
            for m in range(steps):
                here = first + jnp.asarray(m * tile, I16)
                value = jnp.zeros((tile, S), BF16)
                for k in range(TAPS):
                    value = jnp.where(cells[k] == here, weights[k], value)
                start = pl.multiple_of((n * steps + m) * tile, tile)
                out[pl.ds(start, tile), pl.ds(q * S, S)] = value
            return first + jnp.asarray(steps * tile, I16)

        first = lax.broadcasted_iota(I32, (tile, S), 0).astype(I16)
        lax.fori_loop(0, ROWS // (steps * tile), fill, first)


def spread_own_kernel(cells, weights, out):
    spread(
        lambda k, q: cells[pl.ds(k, 1), pl.ds(q * S, S)] - ROWS,
        lambda k, q: weights[pl.ds(k, 1), pl.ds(q * S, S)],
        out,
    )


def spread_pair_kernel(n_cols, gy_e, gy_o, out_e, out_o):
    here, (even, odd, _, _) = partners(n_cols)
    blocks = SENS // S * TAPS
    for partner, arrived, out in ((even, gy_e, out_e), (odd, gy_o, out_o)):
        base = jnp.where(partner > here, 0, 2 * ROWS)
        high = arrived[pl.ds(GX_ROWS, blocks), :].astype(F32).astype(I32)
        low = arrived[pl.ds(GX_ROWS + blocks, blocks), :].astype(F32).astype(I32)
        weight = arrived[pl.ds(GX_ROWS + 2 * blocks, blocks), :].astype(F32)
        cell = high * 128 + low - base
        spread(
            lambda k, q: cell[q * TAPS + k : q * TAPS + k + 1, :],
            lambda k, q: weight[q * TAPS + k : q * TAPS + k + 1, :],
            out,
        )


def final_kernel(
    emission, rho_full, aims, acc_in, gy_e, gy_o, gx_e, gx_o, mix_e, mix_o, mix_own,
    radiosity, part_e, part_o, turned, acc, base, sem_base, sems,
):
    del acc_in, mix_own
    base_copy = pltpu.make_async_copy(emission, base, sem_base)
    base_copy.start()
    add_arrived([aims[n] for n in range(4 * CAP)], (gy_e, gy_o, gx_e, gx_o), acc)
    base_copy.wait()
    copies = []
    for c in range(CL):
        value = radiosity_of(base, rho_full, acc, c)
        acc[c] = value
        copy = pltpu.make_async_copy(acc.at[c], radiosity.at[pl.ds(c * P_SIZE, P_SIZE)], sems.at[c])
        copy.start()
        copies.append(copy)
        turned[:, pl.ds(c * P_SIZE, P_SIZE)] = value.T.astype(BF16)
    part_e[...] = dot(turned[...], mix_e[...]).astype(BF16)
    part_o[...] = dot(turned[...], mix_o[...]).astype(BF16)
    for copy in copies:
        copy.wait()


def own_sensor_kernel(turned, mix, out):
    out[...] = dot(turned[...], mix[...])


def last_kernel(own, part_e, part_o, out):
    total = own[...] + part_e[...].astype(F32) + part_o[...].astype(F32)
    out[...] = total.T


def swap(x, axis, odd):
    size = lax.axis_size(axis)
    pairs = [(i, i + 1) for i in range(odd, size - 1, 2)]
    return lax.ppermute(x, axis, [p for a, b in pairs for p in ((a, b), (b, a))])


def exchange(gy_e, gy_o, gx_e, gx_o):
    sent = (swap(gy_e, "gy", 0), swap(gy_o, "gy", 1), swap(gx_e, "gx", 0), swap(gx_o, "gx", 1))
    return [on_chip(x) for x in sent]


def per_device(
    emission, reflectance, link_blocks, link_source, link_target, link_slot, sensor_cell, sensor_weight
):
    n_cols = lax.axis_size("gy")
    cells, weights = in_hbm(sensor_cell.T), in_hbm(sensor_weight.T)
    flat = in_hbm(emission)
    cube = in_hbm(emission.reshape(CL, P_SIZE, S))
    far = in_hbm(link_blocks)
    links = [in_hbm(x) for x in (link_target.T, link_source, link_slot)]
    one_sem = pltpu.SemaphoreType.DMA
    field_shape = pltpu.VMEM((CL, P_SIZE, S), BF16)
    term_scratch = [
        field_shape,
        pltpu.VMEM((PAIR, P_SIZE, P_SIZE), BF16),
        pltpu.SemaphoreType.DMA((PAIR,)),
        one_sem,
    ]
    base_scratch = [pltpu.VMEM((ROWS, S), BF16), one_sem]
    acc_shape = pltpu.VMEM((CL + 1, P_SIZE, S), F32)
    mix_shape = pltpu.VMEM((ROWS, SENS), BF16)

    def pack_shapes(rows):
        return [pltpu.VMEM((rows, S), BF16)] * 2

    def table(size):
        return jax.ShapeDtypeStruct((size,), I32)

    out_gy_e, out_gy_o, tab_y, weights_sum = pl.pallas_call(
        functools.partial(first_kernel, n_cols),
        out_shape=pack_shapes(GY_ROWS) + [table(128), pltpu.VMEM((TAPS, SENS), F32)],
        in_specs=[SM, SM, SM, ANY, ANY, VM, VM],
        out_specs=[VM, VM, SM, VM],
        scratch_shapes=term_scratch,
        compiler_params=params(16),
        name="gy_terms",
    )(*links, cube, far, cells, weights)
    out_gx_e, out_gx_o, tab_x, own = pl.pallas_call(
        functools.partial(gx_kernel, n_cols),
        out_shape=pack_shapes(GX_ROWS) + [table(128), table(512)],
        in_specs=[SM, SM, SM, ANY, ANY],
        out_specs=[VM, VM, SM, SM],
        scratch_shapes=term_scratch,
        compiler_params=params(16),
        name="gx_terms",
    )(*links, cube, far)
    arrived = exchange(out_gy_e, out_gy_o, out_gx_e, out_gx_o)
    acc, rho_full, near = pl.pallas_call(
        own_first_kernel,
        out_shape=[acc_shape, pltpu.VMEM((ROWS, S), F32), pltpu.VMEM(link_blocks.shape, BF16)],
        in_specs=[SM, ANY, ANY, VM],
        out_specs=[VM, VM, VM],
        scratch_shapes=[field_shape, pltpu.SemaphoreType.DMA((LINKS // CHUNK,)), one_sem],
        compiler_params=params(16),
        name="own_first",
    )(own, far, cube, reflectance.reshape(ROWS // S, S))
    near, rho_full = on_chip(near), on_chip(rho_full)
    mix_own = pl.pallas_call(
        spread_own_kernel,
        out_shape=mix_shape,
        in_specs=[VM, VM],
        out_specs=VM,
        compiler_params=params(16),
        name="spread_own",
    )(cells, on_chip(weights_sum))

    *sent, field, aims, _ = pl.pallas_call(
        second_kernel,
        out_shape=pack_shapes(TERM_ROWS) * 2 + [field_shape, table(4 * CAP), acc_shape],
        in_specs=[SM, SM, VM, ANY] + [VM] * 6,
        out_specs=[VM] * 5 + [SM, VM],
        input_output_aliases={5: 6},
        scratch_shapes=base_scratch,
        compiler_params=params(16),
        name="second_terms",
    )(tab_y, tab_x, near, flat, rho_full, on_chip(acc), *arrived)
    mix_e, mix_o = pl.pallas_call(
        functools.partial(spread_pair_kernel, n_cols),
        out_shape=[mix_shape] * 2,
        in_specs=[VM, VM],
        out_specs=[VM, VM],
        compiler_params=params(16),
        name="spread_pair",
    )(*arrived[:2])
    arrived = exchange(*sent)
    acc = pl.pallas_call(
        own_kernel,
        out_shape=acc_shape,
        in_specs=[SM, VM, VM],
        out_specs=VM,
        compiler_params=params(16),
        name="own_second",
    )(own, near, on_chip(field))

    radiosity, part_e, part_o, turned, _ = pl.pallas_call(
        final_kernel,
        out_shape=[jax.ShapeDtypeStruct((ROWS, S), F32)]
        + [pltpu.VMEM((S, SENS), BF16)] * 2
        + [pltpu.VMEM((S, ROWS), BF16), acc_shape],
        in_specs=[ANY, VM, SM] + [VM] * 7 + [ANY],
        out_specs=[ANY] + [VM] * 4,
        input_output_aliases={3: 4},
        scratch_shapes=base_scratch + [pltpu.SemaphoreType.DMA((CL,))],
        compiler_params=params(16),
        name="final_sum",
    )(
        flat, rho_full, aims, on_chip(acc), *arrived, on_chip(mix_e), on_chip(mix_o), on_chip(mix_own)
    )
    part_e, part_o = swap(part_e, "gy", 0), swap(part_o, "gy", 1)
    own_sum = pl.pallas_call(
        own_sensor_kernel,
        out_shape=pltpu.VMEM((S, SENS), F32),
        in_specs=[VM, VM],
        out_specs=VM,
        compiler_params=params(16),
        name="own_sensors",
    )(on_chip(turned), on_chip(mix_own))
    sensor_values = pl.pallas_call(
        last_kernel,
        out_shape=jax.ShapeDtypeStruct((SENS, S), F32),
        in_specs=[VM, VM, VM],
        out_specs=VM,
        compiler_params=params(16),
        name="sensor_sum",
    )(on_chip(own_sum), on_chip(part_e), on_chip(part_o))
    return radiosity, sensor_values


def solution(mesh):
    spread_axes = P(("gx", "gy"))
    rows = P(("gx", "gy"), None)
    return jax.shard_map(
        per_device,
        mesh=mesh,
        in_specs=(rows, spread_axes, P(("gx", "gy"), None, None), spread_axes, rows, spread_axes, rows, rows),
        out_specs=(rows, rows),
        check_vma=False,
    )
```

profile of v0, /device:TPU:11, one launch (start us, length us, event | category | flops | bytes accessed | tf_op | source)
XLA Modules:
  0.0 74.5 jit_solution(4370143624801295485)
XLA Ops:
  0.6 4.4 %gy_terms.1 = (bf16[2416,128]{1,0:T(8,128)(2,1)S(1)}, bf16[2416,128]{1,0:T(8,128)(2,1)S(1)}, s32[128]{0:T(128)S(1)}, f32[8,512]{1,0:T(8,128)S(1)}) custom-call(s32[1,144]{1,0:T(1,128)} %bitcast.12, s32[144]{0:T(256)} %source.3, s32[144]{0:T(256)} %slot.3, bf16[12,256,128]{2,1,0:T(8,128)(2,1)} %bitcast.6, bf16[144,256,256]{2,1,0:T(8,128)(2,1)} %blocks.3, ...), custom_call_target="tpu_custom_call" | custom-call | tf_op jit(solution)/shard_map/gy_terms/pallas_call | solution.py:391
  5.0 1.7 %collective-permute-start = (bf16[2416,128]{1,0:T(8,128)(2,1)S(1)}, bf16[2416,128]{1,0:T(8,128)(2,1)S(1)}, u32[]{:S(2)}, u32[]{:S(2)}) collective-permute-start(bf16[2416,128]{1,0:T(8,128)(2,1)S(1)} %get-tuple-element.31), channel_id=1, source_target_pairs={{0,1},{1,0},{2,3},{3,2},{4,5},{5,4},{6,7},{7,6},{8,9},{9,8},{10,11... | collective-permute-start | bytes 1855496 | tf_op jit(solution)/shard_map/ppermute | solution.py:356
  6.8 0.0 copy-start
  6.8 4.2 %collective-permute-start.1 = (bf16[2416,128]{1,0:T(8,128)(2,1)S(1)}, bf16[2416,128]{1,0:T(8,128)(2,1)S(1)}, u32[]{:S(2)}, u32[]{:S(2)}) collective-permute-start(bf16[2416,128]{1,0:T(8,128)(2,1)S(1)} %get-tuple-element.32), channel_id=1, source_target_pairs={{1,2},{2,1},{3,4},{4,3},{5,6},{6,5},{7,8},{8,7},{9,10},{10,9},{11,... | collective-permute-start | bytes 1855496 | tf_op jit(solution)/shard_map/ppermute | solution.py:356
  10.9 5.8 %gx_terms.1 = (bf16[2320,128]{1,0:T(8,128)(2,1)S(1)}, bf16[2320,128]{1,0:T(8,128)(2,1)S(1)}, s32[128]{0:T(128)S(1)}, s32[512]{0:T(512)S(1)}) custom-call(s32[1,144]{1,0:T(1,128)} %bitcast.13, s32[144]{0:T(256)} %source.3, s32[144]{0:T(256)} %slot.3, bf16[12,256,128]{2,1,0:T(8,128)(2,1)} %bitcast.7, bf16[144,256,256]{2,1,0:T(8,128)(2,1)} %blocks.3), custom_call_target="tpu_custom_call" | custom-call | tf_op jit(solution)/shard_map/gx_terms/pallas_call | solution.py:400
  16.8 1.8 %collective-permute-start.2 = (bf16[2320,128]{1,0:T(8,128)(2,1)S(1)}, bf16[2320,128]{1,0:T(8,128)(2,1)S(1)}, u32[]{:S(2)}, u32[]{:S(2)}) collective-permute-start(bf16[2320,128]{1,0:T(8,128)(2,1)S(1)} %get-tuple-element.33), channel_id=1, source_target_pairs={{0,16},{16,0},{32,48},{48,32},{64,80},{80,64},{96,112},{112,96},{1... | collective-permute-start | bytes 1781768 | tf_op jit(solution)/shard_map/ppermute | solution.py:356
  18.5 3.5 %collective-permute-start.3 = (bf16[2320,128]{1,0:T(8,128)(2,1)S(1)}, bf16[2320,128]{1,0:T(8,128)(2,1)S(1)}, u32[]{:S(2)}, u32[]{:S(2)}) collective-permute-start(bf16[2320,128]{1,0:T(8,128)(2,1)S(1)} %get-tuple-element.34), channel_id=1, source_target_pairs={{16,32},{32,16},{48,64},{64,48},{80,96},{96,80},{17,33},{33,17},{4... | collective-permute-start | bytes 1781768 | tf_op jit(solution)/shard_map/ppermute | solution.py:356
  22.0 0.0 copy-done
  22.1 12.1 %own_first.1 = (f32[13,256,128]{2,1,0:T(8,128)S(1)}, f32[3072,128]{1,0:T(8,128)S(1)}, bf16[144,256,256]{2,1,0:T(8,128)(2,1)S(1)}) custom-call(s32[512]{0:T(512)S(1)} %get-tuple-element.25.own, bf16[144,256,256]{2,1,0:T(8,128)(2,1)} %blocks.3, bf16[12,256,128]{2,1,0:T(8,128)(2,1)} %bitcast.8, f32[24,128]{1,0:T(8,128)S(1)} %bitcast.5), custom_call_target="tpu_custom_call" | custom-call | tf_op jit(solution)/shard_map/own_first/pallas_call | solution.py:410
  34.1 0.0 collective-permute-done.2.gx_e
  34.1 0.0 collective-permute-done.3.gx_o
  34.2 0.0 collective-permute-done.gy_e
  34.2 0.0 collective-permute-done.1.gy_o
  34.2 3.7 %second_terms.1 = (bf16[2304,128]{1,0:T(8,128)(2,1)S(1)}, bf16[2304,128]{1,0:T(8,128)(2,1)S(1)}, bf16[2304,128]{1,0:T(8,128)(2,1)S(1)}, bf16[2304,128]{1,0:T(8,1...) custom-call(s32[128]{0:T(128)S(1)} %get-tuple-element.27.tab_y, ...), custom_call_target="tpu_custom_call", output_to_operand_aliasing={{6}: (5, {})} | custom-call | tf_op jit(solution)/shard_map/second_terms/pallas_call | solution.py:429
  37.9 1.4 %collective-permute-start.4 = (bf16[2304,128]{1,0:T(8,128)(2,1)S(1)}, bf16[2304,128]{1,0:T(8,128)(2,1)S(1)}, u32[]{:S(2)}, u32[]{:S(2)}) collective-permute-start(bf16[2304,128]{1,0:T(8,128)(2,1)S(1)} %get-tuple-element.37), channel_id=1, source_target_pairs={{0,1},{1,0},{2,3},{3,2},{4,5},{5,4},{6,7},{7,6},{8,9},{9,8},{10,11... | collective-permute-start | bytes 1769480 | tf_op jit(solution)/shard_map/ppermute | solution.py:356
  39.4 2.5 %collective-permute-start.5 = (bf16[2304,128]{1,0:T(8,128)(2,1)S(1)}, bf16[2304,128]{1,0:T(8,128)(2,1)S(1)}, u32[]{:S(2)}, u32[]{:S(2)}) collective-permute-start(bf16[2304,128]{1,0:T(8,128)(2,1)S(1)} %get-tuple-element.38), channel_id=1, source_target_pairs={{1,2},{2,1},{3,4},{4,3},{5,6},{6,5},{7,8},{8,7},{9,10},{10,9},{11,... | collective-permute-start | bytes 1769480 | tf_op jit(solution)/shard_map/ppermute | solution.py:356
  41.8 0.4 collective-permute-start.6
  42.3 2.2 %collective-permute-start.7 = (bf16[2304,128]{1,0:T(8,128)(2,1)S(1)}, bf16[2304,128]{1,0:T(8,128)(2,1)S(1)}, u32[]{:S(2)}, u32[]{:S(2)}) collective-permute-start(bf16[2304,128]{1,0:T(8,128)(2,1)S(1)} %get-tuple-element.40), channel_id=1, source_target_pairs={{16,32},{32,16},{48,64},{64,48},{80,96},{96,80},{17,33},{33,17},{4... | collective-permute-start | bytes 1769480 | tf_op jit(solution)/shard_map/ppermute | solution.py:356
  44.4 2.9 %spread_own.1.mix_own.mix = bf16[3072,512]{1,0:T(8,128)(2,1)S(1)} custom-call(s32[8,512]{1,0:T(8,128)} %bitcast.10, f32[8,512]{1,0:T(8,128)S(1)} %get-tuple-element.43.weights), custom_call_target="tpu_custom_call" | custom-call | tf_op jit(solution)/shard_map/spread_own/pallas_call | solution.py:420
  47.4 6.0 %own_second.1.acc_in = f32[13,256,128]{2,1,0:T(8,128)S(1)} custom-call(s32[512]{0:T(512)S(1)} %get-tuple-element.25.own, bf16[144,256,256]{2,1,0:T(8,128)(2,1)S(1)} %get-tuple-element.29.blocks, bf16[12,256,128]{2,1,0:T(8,128)(2,1)S(1)} %get-tuple-element.36.field), custom_call_target="tpu_custom_call" | custom-call | tf_op jit(solution)/shard_map/own_second/pallas_call | solution.py:448
  53.4 4.5 %spread_pair.1 = (bf16[3072,512]{1,0:T(8,128)(2,1)S(1)}, bf16[3072,512]{1,0:T(8,128)(2,1)S(1)}) custom-call(bf16[2416,128]{1,0:T(8,128)(2,1)S(1)} %collective-permute-done.gy_e, bf16[2416,128]{1,0:T(8,128)(2,1)S(1)} %collective-permute-done.1.gy_o), custom_call_target="tpu_custom_call" | custom-call | tf_op jit(solution)/shard_map/spread_pair/pallas_call | solution.py:439
  57.9 0.0 collective-permute-done.4.gy_e
  57.9 0.1 collective-permute-done.5.gy_o
  58.0 0.0 collective-permute-done.6.gx_e
  58.0 0.0 collective-permute-done.7.gx_o
  58.0 3.8 %final_sum.1 = (f32[3072,128]{1,0:T(8,128)}, bf16[128,512]{1,0:T(8,128)(2,1)S(1)}, bf16[128,512]{1,0:T(8,128)(2,1)S(1)}, bf16[128,3072]{1,0:T(8,128)(2,1)S(1)}, f32[13,256,128]{2,1,0:T(8,128)S(1)}) custom-call(bf16[3072,128]{1,0:T(8,128)(2,1)} %emission.3, f32[3072,128]{1,0:T(8,128)S(1)} %get-tuple-element.26.rho_full, ...), custom_call_target="tpu_custom_call", output_to_operand_aliasing={{4}: (3, {})} | custom-call | tf_op jit(solution)/shard_map/final_sum/pallas_call | solution.py:457
  61.9 2.4 %collective-permute-start.8 = (bf16[128,512]{1,0:T(8,128)(2,1)S(1)}, bf16[128,512]{1,0:T(8,128)(2,1)S(1)}, u32[]{:S(2)}, u32[]{:S(2)}) collective-permute-start(bf16[128,512]{1,0:T(8,128)(2,1)S(1)} %get-tuple-element.46), channel_id=1, source_target_pairs={{0,1},{1,0},{2,3},{3,2},{4,5},{5,4},{6,7},{7,6},{8,9},{9,8},{10,11... | collective-permute-start | bytes 393224 | tf_op jit(solution)/shard_map/ppermute | solution.py:356
  64.2 3.8 %collective-permute-start.9 = (bf16[128,512]{1,0:T(8,128)(2,1)S(1)}, bf16[128,512]{1,0:T(8,128)(2,1)S(1)}, u32[]{:S(2)}, u32[]{:S(2)}) collective-permute-start(bf16[128,512]{1,0:T(8,128)(2,1)S(1)} %get-tuple-element.47), channel_id=1, source_target_pairs={{1,2},{2,1},{3,4},{4,3},{5,6},{6,5},{7,8},{8,7},{9,10},{10,9},{11,... | collective-permute-start | bytes 393224 | tf_op jit(solution)/shard_map/ppermute | solution.py:356
  68.1 0.6 own_sensors.1.own
  68.7 0.0 collective-permute-done.8.part_e
  68.7 5.0 %collective-permute-done.9.part_o = bf16[128,512]{1,0:T(8,128)(2,1)S(1)} collective-permute-done((bf16[128,512]{1,0:T(8,128)(2,1)S(1)}, bf16[128,512]{1,0:T(8,128)(2,1)S(1)}, u32[]{:S(2)}, u32[]{:S(2)}) %collective-permute-start.9) | collective-permute-done | bytes 131104 | tf_op jit(solution)/shard_map/ppermute | solution.py:356
  73.6 0.8 %sensor_sum.1 = f32[512,128]{1,0:T(8,128)} custom-call(f32[128,512]{1,0:T(8,128)S(1)} %own_sensors.1.own, bf16[128,512]{1,0:T(8,128)(2,1)S(1)} %collective-permute-done.8.part_e, bf16[128,512]{1,0:T(8,128)(2,1)S(1)} %collective-permute-done.9.part_o), custom_call_target="tpu_custom_call" | custom-call | tf_op jit(solution)/shard_map/sensor_sum/pallas_call | solution.py:480
Async XLA Ops:
  5.0 29.1 %collective-permute-start = (bf16[2416,128]{1,0:T(8,128)(2,1)S(1)}, bf16[2416,128]{1,0:T(8,128)(2,1)S(1)}, u32[]{:S(2)}, u32[]{:S(2)}) collective-permute-start(bf16[2416,128]{1,0:T(8,128)(2,1)S(1)} %get-tuple-element.31), channel_id=1, source_target_pairs={{0,1},{1,0},{2,3},{3,2},{4,5},{5,4},{6,7},{7,6},{8,9},{9,8},{10,11... | collective-permute-start | bytes 1855496 | tf_op jit(solution)/shard_map/ppermute | solution.py:356
  6.8 15.3 %copy-start = (f32[3072]{0:T(1024)S(1)}, f32[3072]{0:T(1024)}, u32[]{:S(2)}) copy-start(f32[3072]{0:T(1024)} %param.9) | copy-start | bytes 36868
  6.8 27.4 %collective-permute-start.1 = (bf16[2416,128]{1,0:T(8,128)(2,1)S(1)}, bf16[2416,128]{1,0:T(8,128)(2,1)S(1)}, u32[]{:S(2)}, u32[]{:S(2)}) collective-permute-start(bf16[2416,128]{1,0:T(8,128)(2,1)S(1)} %get-tuple-element.32), channel_id=1, source_target_pairs={{1,2},{2,1},{3,4},{4,3},{5,6},{6,5},{7,8},{8,7},{9,10},{10,9},{11,... | collective-permute-start | bytes 1855496 | tf_op jit(solution)/shard_map/ppermute | solution.py:356
  16.8 17.4 %collective-permute-start.2 = (bf16[2320,128]{1,0:T(8,128)(2,1)S(1)}, bf16[2320,128]{1,0:T(8,128)(2,1)S(1)}, u32[]{:S(2)}, u32[]{:S(2)}) collective-permute-start(bf16[2320,128]{1,0:T(8,128)(2,1)S(1)} %get-tuple-element.33), channel_id=1, source_target_pairs={{0,16},{16,0},{32,48},{48,32},{64,80},{80,64},{96,112},{112,96},{1... | collective-permute-start | bytes 1781768 | tf_op jit(solution)/shard_map/ppermute | solution.py:356
  18.5 15.6 %collective-permute-start.3 = (bf16[2320,128]{1,0:T(8,128)(2,1)S(1)}, bf16[2320,128]{1,0:T(8,128)(2,1)S(1)}, u32[]{:S(2)}, u32[]{:S(2)}) collective-permute-start(bf16[2320,128]{1,0:T(8,128)(2,1)S(1)} %get-tuple-element.34), channel_id=1, source_target_pairs={{16,32},{32,16},{48,64},{64,48},{80,96},{96,80},{17,33},{33,17},{4... | collective-permute-start | bytes 1781768 | tf_op jit(solution)/shard_map/ppermute | solution.py:356
  37.9 19.9 %collective-permute-start.4 = (bf16[2304,128]{1,0:T(8,128)(2,1)S(1)}, bf16[2304,128]{1,0:T(8,128)(2,1)S(1)}, u32[]{:S(2)}, u32[]{:S(2)}) collective-permute-start(bf16[2304,128]{1,0:T(8,128)(2,1)S(1)} %get-tuple-element.37), channel_id=1, source_target_pairs={{0,1},{1,0},{2,3},{3,2},{4,5},{5,4},{6,7},{7,6},{8,9},{9,8},{10,11... | collective-permute-start | bytes 1769480 | tf_op jit(solution)/shard_map/ppermute | solution.py:356
  39.4 18.6 %collective-permute-start.5 = (bf16[2304,128]{1,0:T(8,128)(2,1)S(1)}, bf16[2304,128]{1,0:T(8,128)(2,1)S(1)}, u32[]{:S(2)}, u32[]{:S(2)}) collective-permute-start(bf16[2304,128]{1,0:T(8,128)(2,1)S(1)} %get-tuple-element.38), channel_id=1, source_target_pairs={{1,2},{2,1},{3,4},{4,3},{5,6},{6,5},{7,8},{8,7},{9,10},{10,9},{11,... | collective-permute-start | bytes 1769480 | tf_op jit(solution)/shard_map/ppermute | solution.py:356
  41.8 16.2 %collective-permute-start.6 = (bf16[2304,128]{1,0:T(8,128)(2,1)S(1)}, bf16[2304,128]{1,0:T(8,128)(2,1)S(1)}, u32[]{:S(2)}, u32[]{:S(2)}) collective-permute-start(bf16[2304,128]{1,0:T(8,128)(2,1)S(1)} %get-tuple-element.39), channel_id=1, source_target_pairs={{0,16},{16,0},{32,48},{48,32},{64,80},{80,64},{96,112},{112,96},{1... | collective-permute-start | bytes 1769480 | tf_op jit(solution)/shard_map/ppermute | solution.py:356
  42.3 15.7 %collective-permute-start.7 = (bf16[2304,128]{1,0:T(8,128)(2,1)S(1)}, bf16[2304,128]{1,0:T(8,128)(2,1)S(1)}, u32[]{:S(2)}, u32[]{:S(2)}) collective-permute-start(bf16[2304,128]{1,0:T(8,128)(2,1)S(1)} %get-tuple-element.40), channel_id=1, source_target_pairs={{16,32},{32,16},{48,64},{64,48},{80,96},{96,80},{17,33},{33,17},{4... | collective-permute-start | bytes 1769480 | tf_op jit(solution)/shard_map/ppermute | solution.py:356
  61.9 6.8 %collective-permute-start.8 = (bf16[128,512]{1,0:T(8,128)(2,1)S(1)}, bf16[128,512]{1,0:T(8,128)(2,1)S(1)}, u32[]{:S(2)}, u32[]{:S(2)}) collective-permute-start(bf16[128,512]{1,0:T(8,128)(2,1)S(1)} %get-tuple-element.46), channel_id=1, source_target_pairs={{0,1},{1,0},{2,3},{3,2},{4,5},{5,4},{6,7},{7,6},{8,9},{9,8},{10,11... | collective-permute-start | bytes 393224 | tf_op jit(solution)/shard_map/ppermute | solution.py:356
  64.2 9.4 %collective-permute-start.9 = (bf16[128,512]{1,0:T(8,128)(2,1)S(1)}, bf16[128,512]{1,0:T(8,128)(2,1)S(1)}, u32[]{:S(2)}, u32[]{:S(2)}) collective-permute-start(bf16[128,512]{1,0:T(8,128)(2,1)S(1)} %get-tuple-element.47), channel_id=1, source_target_pairs={{1,2},{2,1},{3,4},{4,3},{5,6},{6,5},{7,8},{8,7},{9,10},{10,9},{11,... | collective-permute-start | bytes 393224 | tf_op jit(solution)/shard_map/ppermute | solution.py:356
where the time goes:
time: 75 us; the launch traced here: 74.5 us
  Pallas kernels  44.7 us (60%)
  starting transfers between devices  23.8 us (32%)
  waiting for transfers between devices  5.11 us (7%)
  between operations  0.8 us (1%)
    ppermute x10, starting transfers between devices, swap(): lax.ppermute(x, axis, [p for a, b in pairs for p in ((a, b), (b, a))])  23.8 us
    pallas_call x1, Pallas kernels, per_device(): pl.pallas_call(own_first_kernel, out_shape=[acc_shape, pltpu.VMEM((ROWS,...  12.1 us
    pallas_call x1, Pallas kernels, per_device(): pl.pallas_call(own_kernel, out_shape=acc_shape, in_specs=[SM, VM, VM], ou...  5.98 us
    pallas_call x1, Pallas kernels, per_device(): pl.pallas_call(functools.partial(gx_kernel, n_cols), out_shape=pack_shape...  5.83 us
    ppermute x10, waiting for transfers between devices, swap(): lax.ppermute(x, axis, [p for a, b in pairs for p in ((a, b), (b, a))])  5.11 us
    pallas_call x1, Pallas kernels, per_device(): pl.pallas_call(functools.partial(spread_pair_kernel, n_cols), out_shape=[...  4.48 us
    pallas_call x1, Pallas kernels, per_device(): pl.pallas_call(functools.partial(first_kernel, n_cols), out_shape=pack_sh...  4.41 us
    pallas_call x1, Pallas kernels, per_device(): pl.pallas_call(final_kernel, out_shape=[jax.ShapeDtypeStruct((ROWS, S), F...  3.85 us
  transfers between devices with their start and end apart: 10, of which 2 were waited for; matrix products, arithmetic and copies ran while one was open for 0% of the time, Pallas kernels for 43%

commit v1 on v0

v1 whole, which is shorter than its diff:
```python
import functools

import jax
import jax.numpy as jnp
from jax import lax
from jax.experimental import pallas as pl
from jax.experimental.pallas import tpu as pltpu
from jax.sharding import PartitionSpec as P

BF16, F32, I32, I16 = jnp.bfloat16, jnp.float32, jnp.int32, jnp.int16
P_SIZE = 256
S = 128
CL = 12
SENS = 512
TAPS = 8
LINKS = 144
CAP = 9
ROWS = CL * P_SIZE
TERM_ROWS = CAP * P_SIZE
SLOT_ROWS = 16
META_ROWS = 3 * TAPS * SENS // S
GX_ROWS = TERM_ROWS + SLOT_ROWS
GY_ROWS = GX_ROWS + META_ROWS
PAD = 16
GROUP = 24
OWN_SIZE = 256
MIB = 1 << 20

VM = pl.BlockSpec(memory_space=pltpu.VMEM)
SM = pl.BlockSpec(memory_space=pltpu.SMEM)
ANY = pl.BlockSpec(memory_space=pl.ANY)

PAIR = 2 * CAP
SPARE = 3 * PAIR


def on_chip(x):
    return pltpu.with_memory_space_constraint(x, pltpu.VMEM)


def partners(n_cols):
    i, j = lax.axis_index("gx"), lax.axis_index("gy")
    here = i * n_cols + j
    step_y, step_x = 1 - 2 * (j % 2), 1 - 2 * (i % 2)
    return here, (
        here + step_y,
        here - step_y,
        here + step_x * n_cols,
        here - step_x * n_cols,
    )


def dot(a, b):
    return jnp.dot(a, b, preferred_element_type=F32)


def in_hbm(x):
    return pltpu.with_memory_space_constraint(x, pltpu.HBM)


def in_smem(x):
    return pltpu.with_memory_space_constraint(x, pltpu.SMEM)


def settle(tab, counts, source, slot):
    for p in range(PAIR):
        filled = p % CAP < counts[p // CAP]
        link = jnp.where(filled, tab[p], 0)
        tab[p] = link
        tab[PAIR + p] = source[link]
        tab[2 * PAIR + p] = jnp.where(filled, slot[link] + 1, 0)


def fetch(tab, blocks, buf, sems):
    copies = [pltpu.make_async_copy(blocks.at[tab[p]], buf.at[p], sems.at[p]) for p in range(PAIR)]
    for copy in copies:
        copy.start()
    return copies


def send_terms(tab, block, field, packs, sides=(0, 1)):
    for p in [side * CAP + k for side in sides for k in range(CAP)]:
        term = jnp.where(tab[2 * PAIR + p] > 0, dot(block(p), field[tab[PAIR + p]]), 0.0)
        packs[p // CAP][pl.ds((p % CAP) * P_SIZE, P_SIZE), :] = term.astype(BF16)


def clear_tail(pack, used):
    for row in range(used, pack.shape[0], PAD):
        pack[pl.ds(row, PAD), :] = jnp.zeros((PAD, S), BF16)


def put_slots(tab, packs):
    row = lax.broadcasted_iota(I32, (SLOT_ROWS, S), 0)
    for side in range(2):
        slots = jnp.zeros((SLOT_ROWS, S), I32)
        for k in range(CAP):
            slots = jnp.where(row == k, tab[2 * PAIR + side * CAP + k], slots)
        packs[side][pl.ds(TERM_ROWS, SLOT_ROWS), :] = slots.astype(F32).astype(BF16)


def sensor_rows(cells, weights, weights_sum, packs):
    cell, weight = cells[...], weights[...]
    total = weight
    for shift in range(1, TAPS):
        same = pltpu.roll(cell, shift, 0) == cell
        total = total + jnp.where(same, pltpu.roll(weight, shift, 0), 0.0)
    weights_sum[...] = total
    meta = []
    for part in ((cell >> 7).astype(F32), (cell & 127).astype(F32), total):
        for q in range(SENS // S):
            meta.append(part[:, q * S : (q + 1) * S])
    meta = jnp.concatenate(meta, axis=0).astype(BF16)
    for pack in packs:
        pack[pl.ds(GX_ROWS, META_ROWS), :] = meta


def first_kernel(
    n_cols, target_far, source_far, slot_far, emission, blocks, cells_far, weights_far,
    pack_e, pack_o, tab, weights_sum, target, source, slot, field, cells,
    buf, weights, sems, sem_field, sem_links, sem_sensors,
):
    link_copies = [
        pltpu.make_async_copy(far, near, sem_links.at[n])
        for n, (far, near) in enumerate(
            ((target_far, target), (source_far, source), (slot_far, slot))
        )
    ]
    sensor_copies = [
        pltpu.make_async_copy(cells_far, cells, sem_sensors.at[0]),
        pltpu.make_async_copy(weights_far, weights, sem_sensors.at[1]),
    ]
    field_copy = pltpu.make_async_copy(emission, field, sem_field)
    for copy in (*link_copies, *sensor_copies, field_copy):
        copy.start()
    gy_e, gy_o, _, _ = partners(n_cols)[1]
    for copy in link_copies:
        copy.wait()

    def scan(link, counts):
        owner = target[0, link]
        even, odd = owner == gy_e, owner == gy_o
        tab[jnp.where(even, counts[0], jnp.where(odd, CAP + counts[1], SPARE))] = link
        return counts[0] + even.astype(I32), counts[1] + odd.astype(I32)

    counts = lax.fori_loop(0, LINKS, scan, (jnp.int32(0),) * 2, unroll=8)
    settle(tab, counts, source, slot)
    copies = fetch(tab, blocks, buf, sems)
    packs = (pack_e, pack_o)
    put_slots(tab, packs)
    for copy in sensor_copies:
        copy.wait()
    sensor_rows(cells, weights, weights_sum, packs)
    field_copy.wait()
    clear_tail(pack_o, GY_ROWS)
    for side in range(2):
        for copy in copies[side * CAP : (side + 1) * CAP]:
            copy.wait()
        send_terms(tab, lambda p: buf[p], field, packs, (side,))


def gx_kernel(n_cols, target, source, slot, field, blocks, pack_e, pack_o, tab, own):
    gy_e, gy_o, gx_e, gx_o = partners(n_cols)[1]

    def scan(link, counts):
        owner = target[0, link]
        even, odd = owner == gx_e, owner == gx_o
        other = even | odd | (owner == gy_e) | (owner == gy_o)
        tab[jnp.where(even, counts[0], jnp.where(odd, CAP + counts[1], SPARE))] = link
        own[counts[2]] = link
        return (
            counts[0] + even.astype(I32),
            counts[1] + odd.astype(I32),
            counts[2] + jnp.where(other, 0, 1),
        )

    counts = lax.fori_loop(0, LINKS, scan, (jnp.int32(0),) * 3, unroll=8)
    settle(tab, counts, source, slot)
    packs = (pack_e, pack_o)
    put_slots(tab, packs)
    for k in range(GROUP):
        own[counts[2] + k] = 0
    own[OWN_SIZE - 1] = counts[2]
    send_terms(tab, lambda p: blocks[tab[p]], field, packs)


def gx_second_kernel(tab, blocks, field, pack_e, pack_o):
    send_terms(tab, lambda p: blocks[tab[p]], field, (pack_e, pack_o))


def own_terms(own, source, slot, blocks, field, acc):
    acc[...] = jnp.zeros_like(acc)
    count = own[OWN_SIZE - 1]

    def group(g, _):
        terms = []
        for u in range(GROUP):
            link = own[g * GROUP + u]
            terms.append(dot(blocks[link], field[source[link]]).astype(BF16))
        for u in range(GROUP):
            n = g * GROUP + u
            acc[jnp.where(n < count, slot[own[n]], CL)] += terms[u].astype(F32)
        return 0

    lax.fori_loop(0, (count + GROUP - 1) // GROUP, group, 0)


def own_first_kernel(own, source, slot, blocks, field, rho, acc, rho_full):
    for q in range(ROWS // S):
        wide = jnp.broadcast_to(rho[pl.ds(q, 1), :], (S, S))
        rho_full[pl.ds(q * S, S), :] = wide.T
    own_terms(own, source, slot, blocks, field, acc)


def own_kernel(own, source, slot, blocks, field, acc):
    own_terms(own, source, slot, blocks, field, acc)


def slots_of(arrived):
    out = []
    for ref in arrived:
        values = ref[pl.ds(TERM_ROWS, SLOT_ROWS), :].astype(F32).astype(I32)
        for k in range(CAP):
            value = values[k, 0]
            out.append(jnp.where(value == 0, CL, value - 1))
    return out


def add_arrived(aims, arrived, acc):
    for n, aim in enumerate(aims):
        rows = pl.ds((n % CAP) * P_SIZE, P_SIZE)
        acc[aim] += arrived[n // CAP][rows, :].astype(F32)


def radiosity_of(emission, rho_full, acc, c):
    return emission[c].astype(F32) + rho_full[pl.ds(c * P_SIZE, P_SIZE), :] * acc[c]


def add_slots_kernel(acc_in, first, second, acc, aims_out):
    del acc_in
    aims = slots_of((first, second))
    for n, aim in enumerate(aims):
        aims_out[n] = aim
    add_arrived(aims, (first, second), acc)


def add_kernel(aims, acc_in, first, second, acc):
    del acc_in
    add_arrived([aims[n] for n in range(PAIR)], (first, second), acc)


def second_kernel(
    tab, blocks, emission, rho_full, acc_in, mix_own, gy_e, gy_o,
    pack_e, pack_o, field, aims_out, acc,
):
    del mix_own
    add_slots_kernel(acc_in, gy_e, gy_o, acc, aims_out)
    for c in range(CL):
        field[c] = radiosity_of(emission, rho_full, acc, c).astype(BF16)
    clear_tail(pack_e, TERM_ROWS)
    clear_tail(pack_o, TERM_ROWS)
    send_terms(tab, lambda p: blocks[tab[p]], field, (pack_e, pack_o))


def spread(cell_rows, weight_rows, out):
    tile, steps = 16, 8
    for q in range(SENS // S):
        cells = [jnp.broadcast_to(cell_rows(k, q), (tile, S)).astype(I16) for k in range(TAPS)]
        weights = [jnp.broadcast_to(weight_rows(k, q), (tile, S)).astype(BF16) for k in range(TAPS)]

        def fill(n, first):
            for m in range(steps):
                here = first + jnp.asarray(m * tile, I16)
                value = jnp.zeros((tile, S), BF16)
                for k in range(TAPS):
                    value = jnp.where(cells[k] == here, weights[k], value)
                start = pl.multiple_of((n * steps + m) * tile, tile)
                out[pl.ds(start, tile), pl.ds(q * S, S)] = value
            return first + jnp.asarray(steps * tile, I16)

        first = lax.broadcasted_iota(I32, (tile, S), 0).astype(I16)
        lax.fori_loop(0, ROWS // (steps * tile), fill, first)


def spread_own_kernel(cells, weights, out):
    spread(
        lambda k, q: cells[pl.ds(k, 1), pl.ds(q * S, S)] - ROWS,
        lambda k, q: weights[pl.ds(k, 1), pl.ds(q * S, S)],
        out,
    )


def spread_pair_kernel(n_cols, gy_e, gy_o, out_e, out_o):
    here, (even, odd, _, _) = partners(n_cols)
    blocks = SENS // S * TAPS
    for partner, arrived, out in ((even, gy_e, out_e), (odd, gy_o, out_o)):
        base = jnp.where(partner > here, 0, 2 * ROWS)
        high = arrived[pl.ds(GX_ROWS, blocks), :].astype(F32).astype(I32)
        low = arrived[pl.ds(GX_ROWS + blocks, blocks), :].astype(F32).astype(I32)
        weight = arrived[pl.ds(GX_ROWS + 2 * blocks, blocks), :].astype(F32)
        cell = high * 128 + low - base
        spread(
            lambda k, q: cell[q * TAPS + k : q * TAPS + k + 1, :],
            lambda k, q: weight[q * TAPS + k : q * TAPS + k + 1, :],
            out,
        )


def final_kernel(
    emission, rho_full, aims, acc_in, gy_e, gy_o, mix, radiosity, part, turned, acc
):
    add_kernel(aims, acc_in, gy_e, gy_o, acc)
    for c in range(CL):
        value = radiosity_of(emission, rho_full, acc, c)
        radiosity[pl.ds(c * P_SIZE, P_SIZE), :] = value
        turned[:, pl.ds(c * P_SIZE, P_SIZE)] = value.T.astype(BF16)
    part[...] = dot(turned[...], mix[...]).astype(BF16)


def sensor_kernel(turned, mix, out):
    out[...] = dot(turned[...], mix[...]).astype(out.dtype)


def last_kernel(own, part_e, part_o, out):
    total = own[...] + part_e[...].astype(F32) + part_o[...].astype(F32)
    out[...] = total.T


def swap(x, axis, odd):
    size = lax.axis_size(axis)
    pairs = [(i, i + 1) for i in range(odd, size - 1, 2)]
    return lax.ppermute(x, axis, [p for a, b in pairs for p in ((a, b), (b, a))])


def exchange(axis, even, odd):
    from_odd = swap(odd, axis, 1)
    return [on_chip(swap(even, axis, 0)), on_chip(from_odd)]


def per_device(
    emission, reflectance, link_blocks, link_source, link_target, link_slot, sensor_cell, sensor_weight
):
    n_cols = lax.axis_size("gy")
    sensors_far = in_hbm(sensor_cell.T), in_hbm(sensor_weight.T)
    cube = in_hbm(emission.reshape(CL, P_SIZE, S))
    far, near = in_hbm(link_blocks), on_chip(link_blocks)
    links_far = [in_hbm(x) for x in (link_target.T, link_source, link_slot)]
    field_shape = pltpu.VMEM((CL, P_SIZE, S), BF16)
    acc_shape = pltpu.VMEM((CL + 1, P_SIZE, S), F32)
    mix_shape = pltpu.VMEM((ROWS, SENS), BF16)

    def call(kernel, name, out_shape, in_specs, out_specs, **more):
        return pl.pallas_call(
            kernel,
            out_shape=out_shape,
            in_specs=in_specs,
            out_specs=out_specs,
            compiler_params=pltpu.CompilerParams(vmem_limit_bytes=16 * MIB),
            name=name,
            **more,
        )

    def pack_shapes(even_rows, odd_rows):
        return [pltpu.VMEM((even_rows, S), BF16), pltpu.VMEM((odd_rows, S), BF16)]

    def table(size):
        return pltpu.SMEM((size,), I32)

    out_gy_e, out_gy_o, tab_y, weights_sum, *links, field, cells = call(
        functools.partial(first_kernel, n_cols),
        "gy_terms",
        pack_shapes(GY_ROWS, GY_ROWS + PAD)
        + [table(128), pltpu.VMEM((TAPS, SENS), F32)]
        + [pltpu.SMEM(x.shape, I32) for x in links_far]
        + [field_shape, pltpu.VMEM((TAPS, SENS), I32)],
        [ANY] * 7,
        [VM, VM, SM, VM, SM, SM, SM, VM, VM],
        scratch_shapes=[
            pltpu.VMEM((PAIR, P_SIZE, P_SIZE), BF16),
            pltpu.VMEM((TAPS, SENS), F32),
            pltpu.SemaphoreType.DMA((PAIR,)),
            pltpu.SemaphoreType.DMA,
            pltpu.SemaphoreType.DMA((3,)),
            pltpu.SemaphoreType.DMA((2,)),
        ],
    )(*links_far, cube, far, *sensors_far)
    links, tab_y = [in_smem(x) for x in links], in_smem(tab_y)
    emitted = on_chip(field)
    gy_e, gy_o = exchange("gy", out_gy_e, out_gy_o)
    out_gx_e, out_gx_o, tab_x, own = call(
        functools.partial(gx_kernel, n_cols),
        "gx_terms",
        pack_shapes(GX_ROWS, GX_ROWS) + [table(128), table(OWN_SIZE)],
        [SM, SM, SM, VM, VM],
        [VM, VM, SM, SM],
    )(*links, emitted, near)
    tab_x, own = in_smem(tab_x), in_smem(own)
    gx_e, gx_o = exchange("gx", out_gx_e, out_gx_o)
    acc, rho_full = call(
        own_first_kernel,
        "own_first",
        [acc_shape, pltpu.VMEM((ROWS, S), F32)],
        [SM, SM, SM, VM, VM, VM],
        [VM, VM],
    )(own, *links[1:], near, emitted, reflectance.reshape(ROWS // S, S))
    rho_full = on_chip(rho_full)
    mix_own = call(spread_own_kernel, "spread_own", mix_shape, [VM, VM], VM)(
        on_chip(cells), on_chip(weights_sum)
    )
    mix_own = on_chip(mix_own)
    acc, aims_x = call(
        add_slots_kernel,
        "add_gx_first",
        [acc_shape, table(PAIR)],
        [VM] * 3,
        [VM, SM],
        input_output_aliases={0: 0},
    )(on_chip(acc), gx_e, gx_o)

    out_gy_e, out_gy_o, field, aims_y, _ = call(
        second_kernel,
        "gy_terms_second",
        pack_shapes(TERM_ROWS + PAD, TERM_ROWS + 2 * PAD) + [field_shape, table(PAIR), acc_shape],
        [SM, VM, VM, VM, VM, ANY, VM, VM],
        [VM, VM, VM, SM, VM],
        input_output_aliases={4: 4},
    )(tab_y, near, emitted, rho_full, on_chip(acc), mix_own, gy_e, gy_o)
    field = on_chip(field)
    mix_e, mix_o = call(
        functools.partial(spread_pair_kernel, n_cols), "spread_pair", [mix_shape] * 2, [VM, VM], [VM, VM]
    )(gy_e, gy_o)
    gy_e, gy_o = exchange("gy", out_gy_e, out_gy_o)
    sent = call(
        gx_second_kernel, "gx_terms_second", pack_shapes(TERM_ROWS, TERM_ROWS), [SM, VM, VM], [VM, VM]
    )(tab_x, near, field)
    gx_e, gx_o = exchange("gx", *sent)
    acc = call(own_kernel, "own_second", acc_shape, [SM, SM, SM, VM, VM], VM)(
        own, *links[1:], near, field
    )
    acc = call(
        add_kernel, "add_gx_second", acc_shape, [SM, VM, VM, VM], VM, input_output_aliases={1: 0}
    )(in_smem(aims_x), on_chip(acc), gx_e, gx_o)

    radiosity, part_o, turned, _ = call(
        final_kernel,
        "final_sum",
        [pltpu.VMEM((ROWS, S), F32), pltpu.VMEM((S, SENS), BF16), pltpu.VMEM((S, ROWS), BF16), acc_shape],
        [VM, VM, SM, VM, VM, VM, VM],
        [VM] * 4,
        input_output_aliases={3: 3},
    )(emitted, rho_full, in_smem(aims_y), on_chip(acc), gy_e, gy_o, on_chip(mix_o))
    turned = on_chip(turned)

    def sensor_sums(mix, dtype, name):
        out = call(sensor_kernel, name, pltpu.VMEM((S, SENS), dtype), [VM, VM], VM)(turned, mix)
        return on_chip(out)

    from_o = swap(part_o, "gy", 1)
    from_e = swap(sensor_sums(on_chip(mix_e), BF16, "even_sensors"), "gy", 0)
    sensor_values = call(
        last_kernel, "sensor_sum", jax.ShapeDtypeStruct((SENS, S), F32), [VM, VM, VM], VM
    )(sensor_sums(mix_own, F32, "own_sensors"), on_chip(from_e), on_chip(from_o))
    return radiosity, sensor_values


def solution(mesh):
    spread_axes = P(("gx", "gy"))
    rows = P(("gx", "gy"), None)
    return jax.shard_map(
        per_device,
        mesh=mesh,
        in_specs=(rows, spread_axes, P(("gx", "gy"), None, None), spread_axes, rows, spread_axes, rows, rows),
        out_specs=(rows, rows),
        check_vma=False,
    )
```

time: 75 us -> 59.4 us (0.79)
  the two profiles are of different devices: /device:TPU:11 before, /device:TPU:28 now
where the time goes in v1:
time: 59.4 us; the launch traced here: 58.2 us
  Pallas kernels  29.9 us (50%)
  starting transfers between devices  19.8 us (33%)
  waiting for transfers between devices  6.57 us (11%)
  local copies, waits for them, and re-layouts  1.16 us (2%)
  between operations  0.87 us (1%)
    ppermute x10, starting transfers between devices, swap(): lax.ppermute(x, axis, [p for a, b in pairs for p in ((a, b), (b, a))])  19.8 us
    ppermute x10, waiting for transfers between devices, swap(): lax.ppermute(x, axis, [p for a, b in pairs for p in ((a, b), (b, a))])  6.57 us
    pallas_call x1, Pallas kernels, per_device(): call(own_first_kernel, 'own_first', [acc_shape, pltpu.VMEM((ROWS, S), F32...  5.89 us
    pallas_call x1, Pallas kernels, per_device(): call(own_kernel, 'own_second', acc_shape, [SM, SM, SM, VM, VM], VM)  5.23 us
    pallas_call x1, Pallas kernels, per_device(): call(functools.partial(first_kernel, n_cols), 'gy_terms', pack_shapes(GY_...  4.56 us
    pallas_call x1, Pallas kernels, per_device(): call(functools.partial(spread_pair_kernel, n_cols), 'spread_pair', [mix_s...  4.48 us
    pallas_call x1, Pallas kernels, per_device(): call(spread_own_kernel, 'spread_own', mix_shape, [VM, VM], VM)  2.19 us
    pallas_call x1, Pallas kernels, per_device(): call(functools.partial(gx_kernel, n_cols), 'gx_terms', pack_shapes(GX_ROW...  2.04 us
  transfers between devices with their start and end apart: 10, of which 6 were waited for; matrix products, arithmetic and copies ran while one was open for 2% of the time, Pallas kernels for 38%

profile of v1, /device:TPU:28, one launch (start us, length us, event | category | flops | bytes accessed | tf_op | source)
XLA Modules:
  0.0 58.2 jit_solution(18377545647831627277)
XLA Ops:
  0.6 0.0 copy-start
  0.6 4.6 %gy_terms.1 = (bf16[2416,128]{1,0:T(8,128)(2,1)S(1)}, bf16[2432,128]{1,0:T(8,128)(2,1)S(1)}, s32[128]{0:T(128)S(4)}, f32[8,512]{1,0:T(8,128)S(1)}, s32[1,144]{1,...) custom-call(s32[1,144]{1,0:T(1,128)} %bitcast.9, ...), custom_call_target="tpu_custom_call" | custom-call | tf_op jit(solution)/shard_map/gy_terms/pallas_call | solution.py:368
  5.2 6.6 %collective-permute-start.3 = (bf16[2432,128]{1,0:T(8,128)(2,1)S(1)}, bf16[2432,128]{1,0:T(8,128)(2,1)S(1)}, u32[]{:S(2)}, u32[]{:S(2)}) collective-permute-start(bf16[2432,128]{1,0:T(8,128)(2,1)S(1)} %get-tuple-element.44), channel_id=1, source_target_pairs={{1,2},{2,1},{3,4},{4,3},{5,6},{6,5},{7,8},{8,7},{9,10},{10,9},{11,... | collective-permute-start | bytes 1867784 | tf_op jit(solution)/shard_map/ppermute | solution.py:331
  11.8 0.1 collective-permute-start.2
  11.9 0.0 copy-done
  11.9 2.0 %gx_terms.1 = (bf16[2320,128]{1,0:T(8,128)(2,1)S(1)}, bf16[2320,128]{1,0:T(8,128)(2,1)S(1)}, s32[128]{0:T(128)S(4)}, s32[256]{0:T(256)S(4)}) custom-call(s32[1,144]{1,0:T(1,128)S(4)} %get-tuple-element.31.target, s32[144]{0:T(256)S(4)} %get-tuple-element.32.source, s32[144]{0:T(256)S(4)} %get-tuple-element.33.slot, ...), custom_call_target="tpu_custom_call" | custom-call | tf_op jit(solution)/shard_map/gx_terms/pallas_call | solution.py:389
  14.0 0.0 copy-start.1
  14.0 0.1 collective-permute-start
  14.1 2.2 %collective-permute-start.1 = (bf16[2320,128]{1,0:T(8,128)(2,1)S(1)}, bf16[2320,128]{1,0:T(8,128)(2,1)S(1)}, u32[]{:S(2)}, u32[]{:S(2)}) collective-permute-start(bf16[2320,128]{1,0:T(8,128)(2,1)S(1)} %get-tuple-element.39), channel_id=1, source_target_pairs={{16,32},{32,16},{48,64},{64,48},{80,96},{96,80},{17,33},{33,17},{4... | collective-permute-start | bytes 1781768 | tf_op jit(solution)/shard_map/ppermute | solution.py:331
  16.3 2.2 %spread_own.1.mix_own.mix = bf16[3072,512]{1,0:T(8,128)(2,1)S(1)} custom-call(s32[8,512]{1,0:T(8,128)S(1)} %get-tuple-element.41.cells, f32[8,512]{1,0:T(8,128)S(1)} %get-tuple-element.42.weights), custom_call_target="tpu_custom_call" | custom-call | tf_op jit(solution)/shard_map/spread_own/pallas_call | solution.py:406
  18.5 0.0 copy-done.1
  18.5 5.9 %own_first.1 = (f32[13,256,128]{2,1,0:T(8,128)S(1)}, f32[3072,128]{1,0:T(8,128)S(1)}) custom-call(s32[256]{0:T(256)S(4)} %get-tuple-element.34.own, s32[144]{0:T(256)S(4)} %get-tuple-element.32.source, s32[144]{0:T(256)S(4)} %get-tuple-element.33.slot, bf16[144,256,256]{2,1,0:T(8,128)(2,1)S(1)} %copy-done, ...), custom_call_target="tpu_custom_call" | custom-call | tf_op jit(solution)/shard_map/own_first/pallas_call | solution.py:398
  24.4 0.0 collective-permute-done.first
  24.4 0.9 %collective-permute-done.1.second = bf16[2320,128]{1,0:T(8,128)(2,1)S(1)} collective-permute-done((bf16[2320,128]{1,0:T(8,128)(2,1)S(1)}, bf16[2320,128]{1,0:T(8,128)(2,1)S(1)}, u32[]{:S(2)}, u32[]{:S(2)}) %collective-permute-start.1) | collective-permute-done | bytes 593952 | tf_op jit(solution)/shard_map/ppermute | solution.py:331
  25.3 0.3 add_gx_first.1
  25.6 1.4 %collective-permute-done.2.gy_e = bf16[2416,128]{1,0:T(8,128)(2,1)S(1)} collective-permute-done((bf16[2416,128]{1,0:T(8,128)(2,1)S(1)}, bf16[2416,128]{1,0:T(8,128)(2,1)S(1)}, u32[]{:S(2)}, u32[]{:S(2)}) %collective-permute-start.2) | collective-permute-done | bytes 618528 | tf_op jit(solution)/shard_map/ppermute | solution.py:331
  27.0 0.0 collective-permute-done.3.gy_o
  27.0 1.3 %gy_terms_second.1 = (bf16[2320,128]{1,0:T(8,128)(2,1)S(1)}, bf16[2336,128]{1,0:T(8,128)(2,1)S(1)}, bf16[12,256,128]{2,1,0:T(8,128)(2,1)S(1)}, s32[18]{0:T(128)S(4)}, f32[13,256,128]{2,1,0:T(8,128)S(1)}) custom-call(s32[128]{0:T(128)S(4)} %get-tuple-element.36.tab, bf16[144,256,256]{2,1,0:T(8,128)(2,1)S(1)} %copy-done, ...), custom_call_target="tpu_custom_call", output_to_operand_aliasing={{4}: (4, {})} | custom-call | tf_op jit(solution)/shard_map/gy_terms_second/pallas_call | solution.py:419
  28.4 4.3 %collective-permute-start.7 = (bf16[2336,128]{1,0:T(8,128)(2,1)S(1)}, bf16[2336,128]{1,0:T(8,128)(2,1)S(1)}, u32[]{:S(2)}, u32[]{:S(2)}) collective-permute-start(bf16[2336,128]{1,0:T(8,128)(2,1)S(1)} %get-tuple-element.52), channel_id=1, source_target_pairs={{1,2},{2,1},{3,4},{4,3},{5,6},{6,5},{7,8},{8,7},{9,10},{10,9},{11,... | collective-permute-start | bytes 1794056 | tf_op jit(solution)/shard_map/ppermute | solution.py:331
  32.6 0.1 collective-permute-start.6
  32.7 0.8 %gx_terms_second.1 = (bf16[2304,128]{1,0:T(8,128)(2,1)S(1)}, bf16[2304,128]{1,0:T(8,128)(2,1)S(1)}) custom-call(s32[128]{0:T(128)S(4)} %get-tuple-element.48.tab, bf16[144,256,256]{2,1,0:T(8,128)(2,1)S(1)} %copy-done, bf16[12,256,128]{2,1,0:T(8,128)(2,1)S(1)} %get-tuple-element.47.field), custom_call_target="tpu_custom_call" | custom-call | tf_op jit(solution)/shard_map/gx_terms_second/pallas_call | solution.py:432
  33.5 0.1 collective-permute-start.4
  33.6 2.5 %collective-permute-start.5 = (bf16[2304,128]{1,0:T(8,128)(2,1)S(1)}, bf16[2304,128]{1,0:T(8,128)(2,1)S(1)}, u32[]{:S(2)}, u32[]{:S(2)}) collective-permute-start(bf16[2304,128]{1,0:T(8,128)(2,1)S(1)} %get-tuple-element.50), channel_id=1, source_target_pairs={{16,32},{32,16},{48,64},{64,48},{80,96},{96,80},{17,33},{33,17},{4... | collective-permute-start | bytes 1769480 | tf_op jit(solution)/shard_map/ppermute | solution.py:331
  36.1 5.2 %own_second.1.acc_in = f32[13,256,128]{2,1,0:T(8,128)S(1)} custom-call(s32[256]{0:T(256)S(4)} %get-tuple-element.34.own, s32[144]{0:T(256)S(4)} %get-tuple-element.32.source, s32[144]{0:T(256)S(4)} %get-tuple-element.33.slot, bf16[144,256,256]{2,1,0:T(8,128)(2,1)S(1)} %copy-done, bf16[12,256,128]{2,1,0:T(8,128)(2,1)S(1)} %get-tuple-element.47.field), custom_call_target="tpu_custom_call" | custom-call | tf_op jit(solution)/shard_map/own_second/pallas_call | solution.py:436
  41.4 4.5 %spread_pair.1 = (bf16[3072,512]{1,0:T(8,128)(2,1)S(1)}, bf16[3072,512]{1,0:T(8,128)(2,1)S(1)}) custom-call(bf16[2416,128]{1,0:T(8,128)(2,1)S(1)} %collective-permute-done.2.gy_e, bf16[2432,128]{1,0:T(8,128)(2,1)S(1)} %collective-permute-done.3.gy_o), custom_call_target="tpu_custom_call" | custom-call | tf_op jit(solution)/shard_map/spread_pair/pallas_call | solution.py:428
  45.9 0.0 collective-permute-done.4.first
  45.9 0.0 collective-permute-done.5.second
  45.9 0.2 add_gx_second.1.acc_in
  46.1 0.3 collective-permute-done.6.gy_e
  46.4 0.8 %collective-permute-done.7.gy_o = bf16[2336,128]{1,0:T(8,128)(2,1)S(1)} collective-permute-done((bf16[2336,128]{1,0:T(8,128)(2,1)S(1)}, bf16[2336,128]{1,0:T(8,128)(2,1)S(1)}, u32[]{:S(2)}, u32[]{:S(2)}) %collective-permute-start.7) | collective-permute-done | bytes 598048 | tf_op jit(solution)/shard_map/ppermute | solution.py:331
  47.2 0.9 %final_sum.1 = (f32[3072,128]{1,0:T(8,128)S(1)}, bf16[128,512]{1,0:T(8,128)(2,1)S(1)}, bf16[128,3072]{1,0:T(8,128)(2,1)S(1)}, f32[13,256,128]{2,1,0:T(8,128)S(1)}) custom-call(bf16[12,256,128]{2,1,0:T(8,128)(2,1)S(1)} %get-tuple-element.30.field.emission, f32[3072,128]{1,0:T(8,128)S(1)} %get-tuple-element.35.rho_full, ...), custom_call_target="tpu_custom_call", output_to_operand_aliasing={{3}: (3, {})} | custom-call | tf_op jit(solution)/shard_map/final_sum/pallas_call | solution.py:443
  48.0 3.7 %collective-permute-start.9 = (bf16[128,512]{1,0:T(8,128)(2,1)S(1)}, bf16[128,512]{1,0:T(8,128)(2,1)S(1)}, u32[]{:S(2)}, u32[]{:S(2)}) collective-permute-start(bf16[128,512]{1,0:T(8,128)(2,1)S(1)} %get-tuple-element.57), channel_id=1, source_target_pairs={{1,2},{2,1},{3,4},{4,3},{5,6},{6,5},{7,8},{8,7},{9,10},{10,9},{11,... | collective-permute-start | bytes 393224 | tf_op jit(solution)/shard_map/ppermute | solution.py:331
  51.7 0.6 %even_sensors.1 = bf16[128,512]{1,0:T(8,128)(2,1)S(1)} custom-call(bf16[128,3072]{1,0:T(8,128)(2,1)S(1)} %get-tuple-element.55.turned, bf16[3072,512]{1,0:T(8,128)(2,1)S(1)} %get-tuple-element.56.mix), custom_call_target="tpu_custom_call" | custom-call | tf_op jit(solution)/shard_map/even_sensors/pallas_call | solution.py:454
  52.4 0.1 collective-permute-start.8
  52.4 0.6 own_sensors.1.own
  53.0 1.1 %copy.18 = f32[3072,128]{1,0:T(8,128)} copy(f32[3072,128]{1,0:T(8,128)S(1)} %get-tuple-element.58) | data formatting | bytes 3145728
  54.2 3.0 %collective-permute-done.9.part_o = bf16[128,512]{1,0:T(8,128)(2,1)S(1)} collective-permute-done((bf16[128,512]{1,0:T(8,128)(2,1)S(1)}, bf16[128,512]{1,0:T(8,128)(2,1)S(1)}, u32[]{:S(2)}, u32[]{:S(2)}) %collective-permute-start.9) | collective-permute-done | bytes 131104 | tf_op jit(solution)/shard_map/ppermute | solution.py:331
  57.1 0.3 collective-permute-done.8.part_e
  57.4 0.8 %sensor_sum.1 = f32[512,128]{1,0:T(8,128)} custom-call(f32[128,512]{1,0:T(8,128)S(1)} %own_sensors.1.own, bf16[128,512]{1,0:T(8,128)(2,1)S(1)} %collective-permute-done.8.part_e, bf16[128,512]{1,0:T(8,128)(2,1)S(1)} %collective-permute-done.9.part_o), custom_call_target="tpu_custom_call" | custom-call | tf_op jit(solution)/shard_map/sensor_sum/pallas_call | solution.py:459
Async XLA Ops:
  0.6 11.3 %copy-start = (bf16[144,256,256]{2,1,0:T(8,128)(2,1)S(1)}, bf16[144,256,256]{2,1,0:T(8,128)(2,1)}, u32[]{:S(2)}) copy-start(bf16[144,256,256]{2,1,0:T(8,128)(2,1)} %blocks.11) | copy-start | bytes 56623108
  5.2 21.8 %collective-permute-start.3 = (bf16[2432,128]{1,0:T(8,128)(2,1)S(1)}, bf16[2432,128]{1,0:T(8,128)(2,1)S(1)}, u32[]{:S(2)}, u32[]{:S(2)}) collective-permute-start(bf16[2432,128]{1,0:T(8,128)(2,1)S(1)} %get-tuple-element.44), channel_id=1, source_target_pairs={{1,2},{2,1},{3,4},{4,3},{5,6},{6,5},{7,8},{8,7},{9,10},{10,9},{11,... | collective-permute-start | bytes 1867784 | tf_op jit(solution)/shard_map/ppermute | solution.py:331
  11.8 15.2 %collective-permute-start.2 = (bf16[2416,128]{1,0:T(8,128)(2,1)S(1)}, bf16[2416,128]{1,0:T(8,128)(2,1)S(1)}, u32[]{:S(2)}, u32[]{:S(2)}) collective-permute-start(bf16[2416,128]{1,0:T(8,128)(2,1)S(1)} %get-tuple-element.43), channel_id=1, source_target_pairs={{0,1},{1,0},{2,3},{3,2},{4,5},{5,4},{6,7},{7,6},{8,9},{9,8},{10,11... | collective-permute-start | bytes 1855496 | tf_op jit(solution)/shard_map/ppermute | solution.py:331
  14.0 4.5 %copy-start.1 = (f32[3072]{0:T(1024)S(1)}, f32[3072]{0:T(1024)}, u32[]{:S(2)}) copy-start(f32[3072]{0:T(1024)} %param.9) | copy-start | bytes 36868
  14.0 10.4 %collective-permute-start = (bf16[2320,128]{1,0:T(8,128)(2,1)S(1)}, bf16[2320,128]{1,0:T(8,128)(2,1)S(1)}, u32[]{:S(2)}, u32[]{:S(2)}) collective-permute-start(bf16[2320,128]{1,0:T(8,128)(2,1)S(1)} %get-tuple-element.38), channel_id=1, source_target_pairs={{0,16},{16,0},{32,48},{48,32},{64,80},{80,64},{96,112},{112,96},{1... | collective-permute-start | bytes 1781768 | tf_op jit(solution)/shard_map/ppermute | solution.py:331
  14.1 11.2 %collective-permute-start.1 = (bf16[2320,128]{1,0:T(8,128)(2,1)S(1)}, bf16[2320,128]{1,0:T(8,128)(2,1)S(1)}, u32[]{:S(2)}, u32[]{:S(2)}) collective-permute-start(bf16[2320,128]{1,0:T(8,128)(2,1)S(1)} %get-tuple-element.39), channel_id=1, source_target_pairs={{16,32},{32,16},{48,64},{64,48},{80,96},{96,80},{17,33},{33,17},{4... | collective-permute-start | bytes 1781768 | tf_op jit(solution)/shard_map/ppermute | solution.py:331
  28.4 18.8 %collective-permute-start.7 = (bf16[2336,128]{1,0:T(8,128)(2,1)S(1)}, bf16[2336,128]{1,0:T(8,128)(2,1)S(1)}, u32[]{:S(2)}, u32[]{:S(2)}) collective-permute-start(bf16[2336,128]{1,0:T(8,128)(2,1)S(1)} %get-tuple-element.52), channel_id=1, source_target_pairs={{1,2},{2,1},{3,4},{4,3},{5,6},{6,5},{7,8},{8,7},{9,10},{10,9},{11,... | collective-permute-start | bytes 1794056 | tf_op jit(solution)/shard_map/ppermute | solution.py:331
  32.6 13.7 %collective-permute-start.6 = (bf16[2320,128]{1,0:T(8,128)(2,1)S(1)}, bf16[2320,128]{1,0:T(8,128)(2,1)S(1)}, u32[]{:S(2)}, u32[]{:S(2)}) collective-permute-start(bf16[2320,128]{1,0:T(8,128)(2,1)S(1)} %get-tuple-element.51), channel_id=1, source_target_pairs={{0,1},{1,0},{2,3},{3,2},{4,5},{5,4},{6,7},{7,6},{8,9},{9,8},{10,11... | collective-permute-start | bytes 1781768 | tf_op jit(solution)/shard_map/ppermute | solution.py:331
  33.5 12.4 %collective-permute-start.4 = (bf16[2304,128]{1,0:T(8,128)(2,1)S(1)}, bf16[2304,128]{1,0:T(8,128)(2,1)S(1)}, u32[]{:S(2)}, u32[]{:S(2)}) collective-permute-start(bf16[2304,128]{1,0:T(8,128)(2,1)S(1)} %get-tuple-element.49), channel_id=1, source_target_pairs={{0,16},{16,0},{32,48},{48,32},{64,80},{80,64},{96,112},{112,96},{1... | collective-permute-start | bytes 1769480 | tf_op jit(solution)/shard_map/ppermute | solution.py:331
  33.6 12.3 %collective-permute-start.5 = (bf16[2304,128]{1,0:T(8,128)(2,1)S(1)}, bf16[2304,128]{1,0:T(8,128)(2,1)S(1)}, u32[]{:S(2)}, u32[]{:S(2)}) collective-permute-start(bf16[2304,128]{1,0:T(8,128)(2,1)S(1)} %get-tuple-element.50), channel_id=1, source_target_pairs={{16,32},{32,16},{48,64},{64,48},{80,96},{96,80},{17,33},{33,17},{4... | collective-permute-start | bytes 1769480 | tf_op jit(solution)/shard_map/ppermute | solution.py:331
  48.0 9.1 %collective-permute-start.9 = (bf16[128,512]{1,0:T(8,128)(2,1)S(1)}, bf16[128,512]{1,0:T(8,128)(2,1)S(1)}, u32[]{:S(2)}, u32[]{:S(2)}) collective-permute-start(bf16[128,512]{1,0:T(8,128)(2,1)S(1)} %get-tuple-element.57), channel_id=1, source_target_pairs={{1,2},{2,1},{3,4},{4,3},{5,6},{6,5},{7,8},{8,7},{9,10},{10,9},{11,... | collective-permute-start | bytes 393224 | tf_op jit(solution)/shard_map/ppermute | solution.py:331
  52.4 5.0 %collective-permute-start.8 = (bf16[128,512]{1,0:T(8,128)(2,1)S(1)}, bf16[128,512]{1,0:T(8,128)(2,1)S(1)}, u32[]{:S(2)}, u32[]{:S(2)}) collective-permute-start(bf16[128,512]{1,0:T(8,128)(2,1)S(1)} %even_sensors.1), channel_id=1, source_target_pairs={{0,1},{1,0},{2,3},{3,2},{4,5},{5,4},{6,7},{7,6},{8,9},{9,8},{10,11... | collective-permute-start | bytes 393224 | tf_op jit(solution)/shard_map/ppermute | solution.py:331

commit v2 on v1

--- a/solution.py
+++ b/solution.py
@@ -71,17 +71,20 @@
         tab[2 * PAIR + p] = jnp.where(filled, slot[link] + 1, 0)
 
 
-def fetch(tab, blocks, buf, sems):
-    copies = [pltpu.make_async_copy(blocks.at[tab[p]], buf.at[p], sems.at[p]) for p in range(PAIR)]
+def fetch(tab, side, blocks, buf, sems):
+    copies = [
+        pltpu.make_async_copy(blocks.at[tab[side * CAP + k]], buf.at[k], sems.at[k])
+        for k in range(CAP)
+    ]
     for copy in copies:
-        copy.start()
+        copy.start(priority=1)
     return copies
 
 
 def send_terms(tab, block, field, packs, sides=(0, 1)):
-    for p in [side * CAP + k for side in sides for k in range(CAP)]:
+    for n, p in enumerate(side * CAP + k for side in sides for k in range(CAP)):
         term = jnp.where(tab[2 * PAIR + p] > 0, dot(block(p), field[tab[PAIR + p]]), 0.0)
-        packs[p // CAP][pl.ds((p % CAP) * P_SIZE, P_SIZE), :] = term.astype(BF16)
+        packs[n // CAP][pl.ds((n % CAP) * P_SIZE, P_SIZE), :] = term.astype(BF16)
 
 
 def clear_tail(pack, used):
@@ -89,16 +92,16 @@
         pack[pl.ds(row, PAD), :] = jnp.zeros((PAD, S), BF16)
 
 
-def put_slots(tab, packs):
+def put_slots(tab, packs, sides=(0, 1)):
     row = lax.broadcasted_iota(I32, (SLOT_ROWS, S), 0)
-    for side in range(2):
+    for n, side in enumerate(sides):
         slots = jnp.zeros((SLOT_ROWS, S), I32)
         for k in range(CAP):
             slots = jnp.where(row == k, tab[2 * PAIR + side * CAP + k], slots)
-        packs[side][pl.ds(TERM_ROWS, SLOT_ROWS), :] = slots.astype(F32).astype(BF16)
-
-
-def sensor_rows(cells, weights, weights_sum, packs):
+        packs[n][pl.ds(TERM_ROWS, SLOT_ROWS), :] = slots.astype(F32).astype(BF16)
+
+
+def sensor_rows(cells, weights, weights_sum):
     cell, weight = cells[...], weights[...]
     total = weight
     for shift in range(1, TAPS):
@@ -109,14 +112,12 @@
     for part in ((cell >> 7).astype(F32), (cell & 127).astype(F32), total):
         for q in range(SENS // S):
             meta.append(part[:, q * S : (q + 1) * S])
-    meta = jnp.concatenate(meta, axis=0).astype(BF16)
-    for pack in packs:
-        pack[pl.ds(GX_ROWS, META_ROWS), :] = meta
+    return jnp.concatenate(meta, axis=0).astype(BF16)
 
 
 def first_kernel(
     n_cols, target_far, source_far, slot_far, emission, blocks, cells_far, weights_far,
-    pack_e, pack_o, tab, weights_sum, target, source, slot, field, cells,
+    pack, tab, weights_sum, target, source, slot, field, cells, meta,
     buf, weights, sems, sem_field, sem_links, sem_sensors,
 ):
     link_copies = [
@@ -130,11 +131,10 @@
         pltpu.make_async_copy(weights_far, weights, sem_sensors.at[1]),
     ]
     field_copy = pltpu.make_async_copy(emission, field, sem_field)
-    for copy in (*link_copies, *sensor_copies, field_copy):
-        copy.start()
+    for copy in (*link_copies, field_copy, *sensor_copies):
+        copy.start(priority=1)
     gy_e, gy_o, _, _ = partners(n_cols)[1]
-    for copy in link_copies:
-        copy.wait()
+    link_copies[0].wait()
 
     def scan(link, counts):
         owner = target[0, link]
@@ -142,20 +142,33 @@
         tab[jnp.where(even, counts[0], jnp.where(odd, CAP + counts[1], SPARE))] = link
         return counts[0] + even.astype(I32), counts[1] + odd.astype(I32)
 
-    counts = lax.fori_loop(0, LINKS, scan, (jnp.int32(0),) * 2, unroll=8)
+    counts = lax.fori_loop(0, LINKS, scan, (jnp.int32(0),) * 2, unroll=24)
+    for copy in link_copies[1:]:
+        copy.wait()
     settle(tab, counts, source, slot)
-    copies = fetch(tab, blocks, buf, sems)
-    packs = (pack_e, pack_o)
-    put_slots(tab, packs)
+    copies = fetch(tab, 1, blocks, buf, sems)
+    put_slots(tab, (pack,), (1,))
     for copy in sensor_copies:
         copy.wait()
-    sensor_rows(cells, weights, weights_sum, packs)
+    rows = sensor_rows(cells, weights, weights_sum)
+    meta[...] = rows
+    pack[pl.ds(GX_ROWS, META_ROWS), :] = rows
+    clear_tail(pack, GY_ROWS)
     field_copy.wait()
-    clear_tail(pack_o, GY_ROWS)
-    for side in range(2):
-        for copy in copies[side * CAP : (side + 1) * CAP]:
-            copy.wait()
-        send_terms(tab, lambda p: buf[p], field, packs, (side,))
+    for copy in copies:
+        copy.wait()
+    send_terms(tab, lambda p: buf[p - CAP], field, (pack,), (1,))
+
+
+def even_kernel(tab, blocks, field, meta, pack):
+    put_slots(tab, (pack,), (0,))
+    pack[pl.ds(GX_ROWS, META_ROWS), :] = meta[...]
+    send_terms(tab, lambda p: blocks[tab[p]], field, (pack,), (0,))
+
+
+def even_second_kernel(tab, blocks, field, pack):
+    clear_tail(pack, TERM_ROWS)
+    send_terms(tab, lambda p: blocks[tab[p]], field, (pack,), (0,))
 
 
 def gx_kernel(n_cols, target, source, slot, field, blocks, pack_e, pack_o, tab, own):
@@ -173,7 +186,7 @@
             counts[2] + jnp.where(other, 0, 1),
         )
 
-    counts = lax.fori_loop(0, LINKS, scan, (jnp.int32(0),) * 3, unroll=8)
+    counts = lax.fori_loop(0, LINKS, scan, (jnp.int32(0),) * 3, unroll=24)
     settle(tab, counts, source, slot)
     packs = (pack_e, pack_o)
     put_slots(tab, packs)
@@ -191,17 +204,26 @@
     acc[...] = jnp.zeros_like(acc)
     count = own[OWN_SIZE - 1]
 
-    def group(g, _):
+    def group(first, size):
         terms = []
-        for u in range(GROUP):
-            link = own[g * GROUP + u]
+        for u in range(size):
+            link = own[first + u]
             terms.append(dot(blocks[link], field[source[link]]).astype(BF16))
-        for u in range(GROUP):
-            n = g * GROUP + u
+        for u in range(size):
+            n = first + u
             acc[jnp.where(n < count, slot[own[n]], CL)] += terms[u].astype(F32)
+
+    def whole(g, _):
+        group(g * GROUP, GROUP)
         return 0
 
-    lax.fori_loop(0, (count + GROUP - 1) // GROUP, group, 0)
+    halves = (count + GROUP // 2 - 1) // (GROUP // 2)
+    groups = halves // 2
+    lax.fori_loop(0, groups, whole, 0)
+
+    @pl.when(halves > 2 * groups)
+    def _():
+        group(groups * GROUP, GROUP // 2)
 
 
 def own_first_kernel(own, source, slot, blocks, field, rho, acc, rho_full):
@@ -250,19 +272,18 @@
 
 def second_kernel(
     tab, blocks, emission, rho_full, acc_in, mix_own, gy_e, gy_o,
-    pack_e, pack_o, field, aims_out, acc,
+    pack, field, aims_out, acc,
 ):
     del mix_own
     add_slots_kernel(acc_in, gy_e, gy_o, acc, aims_out)
     for c in range(CL):
         field[c] = radiosity_of(emission, rho_full, acc, c).astype(BF16)
-    clear_tail(pack_e, TERM_ROWS)
-    clear_tail(pack_o, TERM_ROWS)
-    send_terms(tab, lambda p: blocks[tab[p]], field, (pack_e, pack_o))
+    clear_tail(pack, TERM_ROWS)
+    send_terms(tab, lambda p: blocks[tab[p]], field, (pack,), (1,))
 
 
 def spread(cell_rows, weight_rows, out):
-    tile, steps = 16, 8
+    tile, steps = 16, 24
     for q in range(SENS // S):
         cells = [jnp.broadcast_to(cell_rows(k, q), (tile, S)).astype(I16) for k in range(TAPS)]
         weights = [jnp.broadcast_to(weight_rows(k, q), (tile, S)).astype(BF16) for k in range(TAPS)]
@@ -359,25 +380,24 @@
             **more,
         )
 
-    def pack_shapes(even_rows, odd_rows):
-        return [pltpu.VMEM((even_rows, S), BF16), pltpu.VMEM((odd_rows, S), BF16)]
+    def pack_shape(rows):
+        return pltpu.VMEM((rows, S), BF16)
 
     def table(size):
         return pltpu.SMEM((size,), I32)
 
-    out_gy_e, out_gy_o, tab_y, weights_sum, *links, field, cells = call(
+    out_gy_o, tab_y, weights_sum, *links, field, cells, meta = call(
         functools.partial(first_kernel, n_cols),
-        "gy_terms",
-        pack_shapes(GY_ROWS, GY_ROWS + PAD)
-        + [table(128), pltpu.VMEM((TAPS, SENS), F32)]
+        "gy_odd_terms",
+        [pack_shape(GY_ROWS + PAD), table(128), pltpu.VMEM((TAPS, SENS), F32)]
         + [pltpu.SMEM(x.shape, I32) for x in links_far]
-        + [field_shape, pltpu.VMEM((TAPS, SENS), I32)],
+        + [field_shape, pltpu.VMEM((TAPS, SENS), I32), pack_shape(META_ROWS)],
         [ANY] * 7,
-        [VM, VM, SM, VM, SM, SM, SM, VM, VM],
+        [VM, SM, VM, SM, SM, SM, VM, VM, VM],
         scratch_shapes=[
-            pltpu.VMEM((PAIR, P_SIZE, P_SIZE), BF16),
+            pltpu.VMEM((CAP, P_SIZE, P_SIZE), BF16),
             pltpu.VMEM((TAPS, SENS), F32),
-            pltpu.SemaphoreType.DMA((PAIR,)),
+            pltpu.SemaphoreType.DMA((CAP,)),
             pltpu.SemaphoreType.DMA,
             pltpu.SemaphoreType.DMA((3,)),
             pltpu.SemaphoreType.DMA((2,)),
@@ -385,11 +405,14 @@
     )(*links_far, cube, far, *sensors_far)
     links, tab_y = [in_smem(x) for x in links], in_smem(tab_y)
     emitted = on_chip(field)
+    out_gy_e = call(even_kernel, "gy_even_terms", pack_shape(GY_ROWS), [SM, VM, VM, VM], VM)(
+        tab_y, near, emitted, on_chip(meta)
+    )
     gy_e, gy_o = exchange("gy", out_gy_e, out_gy_o)
     out_gx_e, out_gx_o, tab_x, own = call(
         functools.partial(gx_kernel, n_cols),
         "gx_terms",
-        pack_shapes(GX_ROWS, GX_ROWS) + [table(128), table(OWN_SIZE)],
+        [pack_shape(GX_ROWS)] * 2 + [table(128), table(OWN_SIZE)],
         [SM, SM, SM, VM, VM],
         [VM, VM, SM, SM],
     )(*links, emitted, near)
@@ -416,21 +439,24 @@
         input_output_aliases={0: 0},
     )(on_chip(acc), gx_e, gx_o)
 
-    out_gy_e, out_gy_o, field, aims_y, _ = call(
+    out_gy_o, field, aims_y, _ = call(
         second_kernel,
-        "gy_terms_second",
-        pack_shapes(TERM_ROWS + PAD, TERM_ROWS + 2 * PAD) + [field_shape, table(PAIR), acc_shape],
+        "gy_odd_second",
+        [pack_shape(TERM_ROWS + 2 * PAD), field_shape, table(PAIR), acc_shape],
         [SM, VM, VM, VM, VM, ANY, VM, VM],
-        [VM, VM, VM, SM, VM],
-        input_output_aliases={4: 4},
+        [VM, VM, SM, VM],
+        input_output_aliases={4: 3},
     )(tab_y, near, emitted, rho_full, on_chip(acc), mix_own, gy_e, gy_o)
     field = on_chip(field)
     mix_e, mix_o = call(
         functools.partial(spread_pair_kernel, n_cols), "spread_pair", [mix_shape] * 2, [VM, VM], [VM, VM]
     )(gy_e, gy_o)
+    out_gy_e = call(
+        even_second_kernel, "gy_even_second", pack_shape(TERM_ROWS + PAD), [SM, VM, VM], VM
+    )(tab_y, near, field)
     gy_e, gy_o = exchange("gy", out_gy_e, out_gy_o)
     sent = call(
-        gx_second_kernel, "gx_terms_second", pack_shapes(TERM_ROWS, TERM_ROWS), [SM, VM, VM], [VM, VM]
+        gx_second_kernel, "gx_second", [pack_shape(TERM_ROWS)] * 2, [SM, VM, VM], [VM, VM]
     )(tab_x, near, field)
     gx_e, gx_o = exchange("gx", *sent)
     acc = call(own_kernel, "own_second", acc_shape, [SM, SM, SM, VM, VM], VM)(

time: 59.4 us -> 58.6 us (0.987)
    pallas_call x4 -> x6, Pallas kernels: 8.7 us -> 8.58 us  [the longest x1 3.91 us: per_device(): call(functools.partial(first_kernel, n_cols), 'gy_odd_terms', [pack_shape...]
  transfers between devices with their start and end apart: 10 -> 10, of which waited for: 6 -> 6; matrix products, arithmetic and copies ran while one was open for 2% -> 2% of each run, Pallas kernels for 38% -> 39%
where the time goes in v2:
time: 58.6 us; the launch traced here: 58 us
  Pallas kernels  29.4 us (50%)
  starting transfers between devices  19.8 us (34%)
  waiting for transfers between devices  6.8 us (12%)
  local copies, waits for them, and re-layouts  1.16 us (2%)
  between operations  0.88 us (2%)
    ppermute x10, starting transfers between devices, swap(): lax.ppermute(x, axis, [p for a, b in pairs for p in ((a, b), (b, a))])  19.8 us
    ppermute x10, waiting for transfers between devices, swap(): lax.ppermute(x, axis, [p for a, b in pairs for p in ((a, b), (b, a))])  6.8 us
    pallas_call x1, Pallas kernels, per_device(): call(own_first_kernel, 'own_first', [acc_shape, pltpu.VMEM((ROWS, S), F32...  5.9 us
    pallas_call x1, Pallas kernels, per_device(): call(own_kernel, 'own_second', acc_shape, [SM, SM, SM, VM, VM], VM)  5.26 us
    pallas_call x1, Pallas kernels, per_device(): call(functools.partial(spread_pair_kernel, n_cols), 'spread_pair', [mix_s...  4.08 us
    pallas_call x1, Pallas kernels, per_device(): call(functools.partial(first_kernel, n_cols), 'gy_odd_terms', [pack_shape...  3.91 us
    pallas_call x1, Pallas kernels, per_device(): call(spread_own_kernel, 'spread_own', mix_shape, [VM, VM], VM)  2.03 us
    pallas_call x1, Pallas kernels, per_device(): call(functools.partial(gx_kernel, n_cols), 'gx_terms', [pack_shape(GX_ROW...  1.97 us
  transfers between devices with their start and end apart: 10, of which 6 were waited for; matrix products, arithmetic and copies ran while one was open for 2% of the time, Pallas kernels for 39%

profile of v2, /device:TPU:28, one launch (start us, length us, event | category | flops | bytes accessed | tf_op | source)
XLA Modules:
  0.0 58.0 jit_solution(2654894080234227993)
XLA Ops:
  0.6 0.0 copy-start
  0.6 3.9 %gy_odd_terms.1 = (bf16[2432,128]{1,0:T(8,128)(2,1)S(1)}, s32[128]{0:T(128)S(4)}, f32[8,512]{1,0:T(8,128)S(1)}, s32[1,144]{1,0:T(1,128)S(4)}, s32[144]{0:T(256)S...) custom-call(s32[1,144]{1,0:T(1,128)} %bitcast.9, ...), custom_call_target="tpu_custom_call" | custom-call | tf_op jit(solution)/shard_map/gy_odd_terms/pallas_call | solution.py:389
  4.6 6.4 %collective-permute-start.3 = (bf16[2432,128]{1,0:T(8,128)(2,1)S(1)}, bf16[2432,128]{1,0:T(8,128)(2,1)S(1)}, u32[]{:S(2)}, u32[]{:S(2)}) collective-permute-start(bf16[2432,128]{1,0:T(8,128)(2,1)S(1)} %get-tuple-element.43), channel_id=1, source_target_pairs={{1,2},{2,1},{3,4},{4,3},{5,6},{6,5},{7,8},{8,7},{9,10},{10,9},{11,... | collective-permute-start | bytes 1867784 | tf_op jit(solution)/shard_map/ppermute | solution.py:352
  11.0 0.0 copy-done
  11.0 0.5 gy_even_terms.1
  11.4 0.1 collective-permute-start.2
  11.5 2.0 %gx_terms.1 = (bf16[2320,128]{1,0:T(8,128)(2,1)S(1)}, bf16[2320,128]{1,0:T(8,128)(2,1)S(1)}, s32[128]{0:T(128)S(4)}, s32[256]{0:T(256)S(4)}) custom-call(s32[1,144]{1,0:T(1,128)S(4)} %get-tuple-element.30.target, s32[144]{0:T(256)S(4)} %get-tuple-element.31.source, s32[144]{0:T(256)S(4)} %get-tuple-element.32.slot, ...), custom_call_target="tpu_custom_call" | custom-call | tf_op jit(solution)/shard_map/gx_terms/pallas_call | solution.py:412
  13.5 0.0 copy-start.1
  13.5 0.1 collective-permute-start
  13.6 2.5 %collective-permute-start.1 = (bf16[2320,128]{1,0:T(8,128)(2,1)S(1)}, bf16[2320,128]{1,0:T(8,128)(2,1)S(1)}, u32[]{:S(2)}, u32[]{:S(2)}) collective-permute-start(bf16[2320,128]{1,0:T(8,128)(2,1)S(1)} %get-tuple-element.38), channel_id=1, source_target_pairs={{16,32},{32,16},{48,64},{64,48},{80,96},{96,80},{17,33},{33,17},{4... | collective-permute-start | bytes 1781768 | tf_op jit(solution)/shard_map/ppermute | solution.py:352
  16.2 2.0 %spread_own.1.mix_own.mix = bf16[3072,512]{1,0:T(8,128)(2,1)S(1)} custom-call(s32[8,512]{1,0:T(8,128)S(1)} %get-tuple-element.40.cells, f32[8,512]{1,0:T(8,128)S(1)} %get-tuple-element.41.weights), custom_call_target="tpu_custom_call" | custom-call | tf_op jit(solution)/shard_map/spread_own/pallas_call | solution.py:429
  18.2 0.0 copy-done.1
  18.2 5.9 %own_first.1 = (f32[13,256,128]{2,1,0:T(8,128)S(1)}, f32[3072,128]{1,0:T(8,128)S(1)}) custom-call(s32[256]{0:T(256)S(4)} %get-tuple-element.33.own, s32[144]{0:T(256)S(4)} %get-tuple-element.31.source, s32[144]{0:T(256)S(4)} %get-tuple-element.32.slot, bf16[144,256,256]{2,1,0:T(8,128)(2,1)S(1)} %copy-done, ...), custom_call_target="tpu_custom_call" | custom-call | tf_op jit(solution)/shard_map/own_first/pallas_call | solution.py:421
  24.1 0.0 collective-permute-done.first
  24.1 0.7 %collective-permute-done.1.second = bf16[2320,128]{1,0:T(8,128)(2,1)S(1)} collective-permute-done((bf16[2320,128]{1,0:T(8,128)(2,1)S(1)}, bf16[2320,128]{1,0:T(8,128)(2,1)S(1)}, u32[]{:S(2)}, u32[]{:S(2)}) %collective-permute-start.1) | collective-permute-done | bytes 593952 | tf_op jit(solution)/shard_map/ppermute | solution.py:352
  24.9 0.3 add_gx_first.1
  25.1 1.8 %collective-permute-done.2.gy_e = bf16[2416,128]{1,0:T(8,128)(2,1)S(1)} collective-permute-done((bf16[2416,128]{1,0:T(8,128)(2,1)S(1)}, bf16[2416,128]{1,0:T(8,128)(2,1)S(1)}, u32[]{:S(2)}, u32[]{:S(2)}) %collective-permute-start.2) | collective-permute-done | bytes 618528 | tf_op jit(solution)/shard_map/ppermute | solution.py:352
  26.9 0.0 collective-permute-done.3.gy_o
  26.9 1.0 %gy_odd_second.1 = (bf16[2336,128]{1,0:T(8,128)(2,1)S(1)}, bf16[12,256,128]{2,1,0:T(8,128)(2,1)S(1)}, s32[18]{0:T(128)S(4)}, f32[13,256,128]{2,1,0:T(8,128)S(1)}) custom-call(s32[128]{0:T(128)S(4)} %get-tuple-element.35.tab, bf16[144,256,256]{2,1,0:T(8,128)(2,1)S(1)} %copy-done, ...), custom_call_target="tpu_custom_call", output_to_operand_aliasing={{3}: (4, {})} | custom-call | tf_op jit(solution)/shard_map/gy_odd_second/pallas_call | solution.py:442
  27.9 3.8 %collective-permute-start.7 = (bf16[2336,128]{1,0:T(8,128)(2,1)S(1)}, bf16[2336,128]{1,0:T(8,128)(2,1)S(1)}, u32[]{:S(2)}, u32[]{:S(2)}) collective-permute-start(bf16[2336,128]{1,0:T(8,128)(2,1)S(1)} %get-tuple-element.50), channel_id=1, source_target_pairs={{1,2},{2,1},{3,4},{4,3},{5,6},{6,5},{7,8},{8,7},{9,10},{10,9},{11,... | collective-permute-start | bytes 1794056 | tf_op jit(solution)/shard_map/ppermute | solution.py:352
  31.7 0.5 gy_even_second.1
  32.2 0.1 collective-permute-start.6
  32.3 0.8 %gx_second.1 = (bf16[2304,128]{1,0:T(8,128)(2,1)S(1)}, bf16[2304,128]{1,0:T(8,128)(2,1)S(1)}) custom-call(s32[128]{0:T(128)S(4)} %get-tuple-element.47.tab, bf16[144,256,256]{2,1,0:T(8,128)(2,1)S(1)} %copy-done, bf16[12,256,128]{2,1,0:T(8,128)(2,1)S(1)} %get-tuple-element.46.field), custom_call_target="tpu_custom_call" | custom-call | tf_op jit(solution)/shard_map/gx_second/pallas_call | solution.py:458
  33.1 0.1 collective-permute-start.4
  33.2 2.5 %collective-permute-start.5 = (bf16[2304,128]{1,0:T(8,128)(2,1)S(1)}, bf16[2304,128]{1,0:T(8,128)(2,1)S(1)}, u32[]{:S(2)}, u32[]{:S(2)}) collective-permute-start(bf16[2304,128]{1,0:T(8,128)(2,1)S(1)} %get-tuple-element.49), channel_id=1, source_target_pairs={{16,32},{32,16},{48,64},{64,48},{80,96},{96,80},{17,33},{33,17},{4... | collective-permute-start | bytes 1769480 | tf_op jit(solution)/shard_map/ppermute | solution.py:352
  35.7 5.3 %own_second.1.acc_in = f32[13,256,128]{2,1,0:T(8,128)S(1)} custom-call(s32[256]{0:T(256)S(4)} %get-tuple-element.33.own, s32[144]{0:T(256)S(4)} %get-tuple-element.31.source, s32[144]{0:T(256)S(4)} %get-tuple-element.32.slot, bf16[144,256,256]{2,1,0:T(8,128)(2,1)S(1)} %copy-done, bf16[12,256,128]{2,1,0:T(8,128)(2,1)S(1)} %get-tuple-element.46.field), custom_call_target="tpu_custom_call" | custom-call | tf_op jit(solution)/shard_map/own_second/pallas_call | solution.py:462
  41.0 4.1 %spread_pair.1 = (bf16[3072,512]{1,0:T(8,128)(2,1)S(1)}, bf16[3072,512]{1,0:T(8,128)(2,1)S(1)}) custom-call(bf16[2416,128]{1,0:T(8,128)(2,1)S(1)} %collective-permute-done.2.gy_e, bf16[2432,128]{1,0:T(8,128)(2,1)S(1)} %collective-permute-done.3.gy_o), custom_call_target="tpu_custom_call" | custom-call | tf_op jit(solution)/shard_map/spread_pair/pallas_call | solution.py:451
  45.1 0.0 collective-permute-done.4.first
  45.1 0.0 collective-permute-done.5.second
  45.1 0.2 add_gx_second.1.acc_in
  45.3 1.0 %collective-permute-done.6.gy_e = bf16[2320,128]{1,0:T(8,128)(2,1)S(1)} collective-permute-done((bf16[2320,128]{1,0:T(8,128)(2,1)S(1)}, bf16[2320,128]{1,0:T(8,128)(2,1)S(1)}, u32[]{:S(2)}, u32[]{:S(2)}) %collective-permute-start.6) | collective-permute-done | bytes 593952 | tf_op jit(solution)/shard_map/ppermute | solution.py:352
  46.3 0.1 collective-permute-done.7.gy_o
  46.4 1.0 %final_sum.1 = (f32[3072,128]{1,0:T(8,128)S(1)}, bf16[128,512]{1,0:T(8,128)(2,1)S(1)}, bf16[128,3072]{1,0:T(8,128)(2,1)S(1)}, f32[13,256,128]{2,1,0:T(8,128)S(1)}) custom-call(bf16[12,256,128]{2,1,0:T(8,128)(2,1)S(1)} %get-tuple-element.29.field.emission, f32[3072,128]{1,0:T(8,128)S(1)} %get-tuple-element.34.rho_full, ...), custom_call_target="tpu_custom_call", output_to_operand_aliasing={{3}: (3, {})} | custom-call | tf_op jit(solution)/shard_map/final_sum/pallas_call | solution.py:469
  47.4 4.1 %collective-permute-start.9 = (bf16[128,512]{1,0:T(8,128)(2,1)S(1)}, bf16[128,512]{1,0:T(8,128)(2,1)S(1)}, u32[]{:S(2)}, u32[]{:S(2)}) collective-permute-start(bf16[128,512]{1,0:T(8,128)(2,1)S(1)} %get-tuple-element.55), channel_id=1, source_target_pairs={{1,2},{2,1},{3,4},{4,3},{5,6},{6,5},{7,8},{8,7},{9,10},{10,9},{11,... | collective-permute-start | bytes 393224 | tf_op jit(solution)/shard_map/ppermute | solution.py:352
  51.5 0.6 %even_sensors.1 = bf16[128,512]{1,0:T(8,128)(2,1)S(1)} custom-call(bf16[128,3072]{1,0:T(8,128)(2,1)S(1)} %get-tuple-element.53.turned, bf16[3072,512]{1,0:T(8,128)(2,1)S(1)} %get-tuple-element.54.mix), custom_call_target="tpu_custom_call" | custom-call | tf_op jit(solution)/shard_map/even_sensors/pallas_call | solution.py:480
  52.1 0.1 collective-permute-start.8
  52.2 0.6 own_sensors.1.own
  52.8 1.1 %copy.18 = f32[3072,128]{1,0:T(8,128)} copy(f32[3072,128]{1,0:T(8,128)S(1)} %get-tuple-element.56) | data formatting | bytes 3145728
  54.0 2.5 %collective-permute-done.9.part_o = bf16[128,512]{1,0:T(8,128)(2,1)S(1)} collective-permute-done((bf16[128,512]{1,0:T(8,128)(2,1)S(1)}, bf16[128,512]{1,0:T(8,128)(2,1)S(1)}, u32[]{:S(2)}, u32[]{:S(2)}) %collective-permute-start.9) | collective-permute-done | bytes 131104 | tf_op jit(solution)/shard_map/ppermute | solution.py:352
  56.5 0.7 %collective-permute-done.8.part_e = bf16[128,512]{1,0:T(8,128)(2,1)S(1)} collective-permute-done((bf16[128,512]{1,0:T(8,128)(2,1)S(1)}, bf16[128,512]{1,0:T(8,128)(2,1)S(1)}, u32[]{:S(2)}, u32[]{:S(2)}) %collective-permute-start.8) | collective-permute-done | bytes 131104 | tf_op jit(solution)/shard_map/ppermute | solution.py:352
  57.2 0.8 %sensor_sum.1 = f32[512,128]{1,0:T(8,128)} custom-call(f32[128,512]{1,0:T(8,128)S(1)} %own_sensors.1.own, bf16[128,512]{1,0:T(8,128)(2,1)S(1)} %collective-permute-done.8.part_e, bf16[128,512]{1,0:T(8,128)(2,1)S(1)} %collective-permute-done.9.part_o), custom_call_target="tpu_custom_call" | custom-call | tf_op jit(solution)/shard_map/sensor_sum/pallas_call | solution.py:485
Async XLA Ops:
  0.6 10.3 %copy-start = (bf16[144,256,256]{2,1,0:T(8,128)(2,1)S(1)}, bf16[144,256,256]{2,1,0:T(8,128)(2,1)}, u32[]{:S(2)}) copy-start(bf16[144,256,256]{2,1,0:T(8,128)(2,1)} %blocks.15) | copy-start | bytes 56623108
  4.6 22.4 %collective-permute-start.3 = (bf16[2432,128]{1,0:T(8,128)(2,1)S(1)}, bf16[2432,128]{1,0:T(8,128)(2,1)S(1)}, u32[]{:S(2)}, u32[]{:S(2)}) collective-permute-start(bf16[2432,128]{1,0:T(8,128)(2,1)S(1)} %get-tuple-element.43), channel_id=1, source_target_pairs={{1,2},{2,1},{3,4},{4,3},{5,6},{6,5},{7,8},{8,7},{9,10},{10,9},{11,... | collective-permute-start | bytes 1867784 | tf_op jit(solution)/shard_map/ppermute | solution.py:352
  11.4 15.5 %collective-permute-start.2 = (bf16[2416,128]{1,0:T(8,128)(2,1)S(1)}, bf16[2416,128]{1,0:T(8,128)(2,1)S(1)}, u32[]{:S(2)}, u32[]{:S(2)}) collective-permute-start(bf16[2416,128]{1,0:T(8,128)(2,1)S(1)} %gy_even_terms.1), channel_id=1, source_target_pairs={{0,1},{1,0},{2,3},{3,2},{4,5},{5,4},{6,7},{7,6},{8,9},{9,8},{10,11... | collective-permute-start | bytes 1855496 | tf_op jit(solution)/shard_map/ppermute | solution.py:352
  13.5 4.7 %copy-start.1 = (f32[3072]{0:T(1024)S(1)}, f32[3072]{0:T(1024)}, u32[]{:S(2)}) copy-start(f32[3072]{0:T(1024)} %param.9) | copy-start | bytes 36868
  13.5 10.6 %collective-permute-start = (bf16[2320,128]{1,0:T(8,128)(2,1)S(1)}, bf16[2320,128]{1,0:T(8,128)(2,1)S(1)}, u32[]{:S(2)}, u32[]{:S(2)}) collective-permute-start(bf16[2320,128]{1,0:T(8,128)(2,1)S(1)} %get-tuple-element.37), channel_id=1, source_target_pairs={{0,16},{16,0},{32,48},{48,32},{64,80},{80,64},{96,112},{112,96},{1... | collective-permute-start | bytes 1781768 | tf_op jit(solution)/shard_map/ppermute | solution.py:352
  13.6 11.2 %collective-permute-start.1 = (bf16[2320,128]{1,0:T(8,128)(2,1)S(1)}, bf16[2320,128]{1,0:T(8,128)(2,1)S(1)}, u32[]{:S(2)}, u32[]{:S(2)}) collective-permute-start(bf16[2320,128]{1,0:T(8,128)(2,1)S(1)} %get-tuple-element.38), channel_id=1, source_target_pairs={{16,32},{32,16},{48,64},{64,48},{80,96},{96,80},{17,33},{33,17},{4... | collective-permute-start | bytes 1781768 | tf_op jit(solution)/shard_map/ppermute | solution.py:352
  27.9 18.4 %collective-permute-start.7 = (bf16[2336,128]{1,0:T(8,128)(2,1)S(1)}, bf16[2336,128]{1,0:T(8,128)(2,1)S(1)}, u32[]{:S(2)}, u32[]{:S(2)}) collective-permute-start(bf16[2336,128]{1,0:T(8,128)(2,1)S(1)} %get-tuple-element.50), channel_id=1, source_target_pairs={{1,2},{2,1},{3,4},{4,3},{5,6},{6,5},{7,8},{8,7},{9,10},{10,9},{11,... | collective-permute-start | bytes 1794056 | tf_op jit(solution)/shard_map/ppermute | solution.py:352
  32.2 14.1 %collective-permute-start.6 = (bf16[2320,128]{1,0:T(8,128)(2,1)S(1)}, bf16[2320,128]{1,0:T(8,128)(2,1)S(1)}, u32[]{:S(2)}, u32[]{:S(2)}) collective-permute-start(bf16[2320,128]{1,0:T(8,128)(2,1)S(1)} %gy_even_second.1), channel_id=1, source_target_pairs={{0,1},{1,0},{2,3},{3,2},{4,5},{5,4},{6,7},{7,6},{8,9},{9,8},{10,11... | collective-permute-start | bytes 1781768 | tf_op jit(solution)/shard_map/ppermute | solution.py:352
  33.1 12.0 %collective-permute-start.4 = (bf16[2304,128]{1,0:T(8,128)(2,1)S(1)}, bf16[2304,128]{1,0:T(8,128)(2,1)S(1)}, u32[]{:S(2)}, u32[]{:S(2)}) collective-permute-start(bf16[2304,128]{1,0:T(8,128)(2,1)S(1)} %get-tuple-element.48), channel_id=1, source_target_pairs={{0,16},{16,0},{32,48},{48,32},{64,80},{80,64},{96,112},{112,96},{1... | collective-permute-start | bytes 1769480 | tf_op jit(solution)/shard_map/ppermute | solution.py:352
  33.2 11.9 %collective-permute-start.5 = (bf16[2304,128]{1,0:T(8,128)(2,1)S(1)}, bf16[2304,128]{1,0:T(8,128)(2,1)S(1)}, u32[]{:S(2)}, u32[]{:S(2)}) collective-permute-start(bf16[2304,128]{1,0:T(8,128)(2,1)S(1)} %get-tuple-element.49), channel_id=1, source_target_pairs={{16,32},{32,16},{48,64},{64,48},{80,96},{96,80},{17,33},{33,17},{4... | collective-permute-start | bytes 1769480 | tf_op jit(solution)/shard_map/ppermute | solution.py:352
  47.4 9.1 %collective-permute-start.9 = (bf16[128,512]{1,0:T(8,128)(2,1)S(1)}, bf16[128,512]{1,0:T(8,128)(2,1)S(1)}, u32[]{:S(2)}, u32[]{:S(2)}) collective-permute-start(bf16[128,512]{1,0:T(8,128)(2,1)S(1)} %get-tuple-element.55), channel_id=1, source_target_pairs={{1,2},{2,1},{3,4},{4,3},{5,6},{6,5},{7,8},{8,7},{9,10},{10,9},{11,... | collective-permute-start | bytes 393224 | tf_op jit(solution)/shard_map/ppermute | solution.py:352
  52.1 5.0 %collective-permute-start.8 = (bf16[128,512]{1,0:T(8,128)(2,1)S(1)}, bf16[128,512]{1,0:T(8,128)(2,1)S(1)}, u32[]{:S(2)}, u32[]{:S(2)}) collective-permute-start(bf16[128,512]{1,0:T(8,128)(2,1)S(1)} %even_sensors.1), channel_id=1, source_target_pairs={{0,1},{1,0},{2,3},{3,2},{4,5},{5,4},{6,7},{7,6},{8,9},{9,8},{10,11... | collective-permute-start | bytes 393224 | tf_op jit(solution)/shard_map/ppermute | solution.py:352

commit v3 on v2

--- a/solution.py
+++ b/solution.py
@@ -21,7 +21,8 @@
 META_ROWS = 3 * TAPS * SENS // S
 GX_ROWS = TERM_ROWS + SLOT_ROWS
 GY_ROWS = GX_ROWS + META_ROWS
-PAD = 16
+PAD = 8
+TAIL = 8
 GROUP = 24
 OWN_SIZE = 256
 MIB = 1 << 20
@@ -327,22 +328,24 @@
 
 
 def final_kernel(
-    emission, rho_full, aims, acc_in, gy_e, gy_o, mix, radiosity, part, turned, acc
+    emission, rho_full, aims, acc_in, gy_e, gy_o, mix_e, mix_o, radiosity, part_e, part_o, turned, acc
 ):
     add_kernel(aims, acc_in, gy_e, gy_o, acc)
     for c in range(CL):
         value = radiosity_of(emission, rho_full, acc, c)
         radiosity[pl.ds(c * P_SIZE, P_SIZE), :] = value
         turned[:, pl.ds(c * P_SIZE, P_SIZE)] = value.T.astype(BF16)
-    part[...] = dot(turned[...], mix[...]).astype(BF16)
+    part_o[pl.ds(0, S), :] = dot(turned[...], mix_o[...]).astype(BF16)
+    part_o[pl.ds(S, TAIL), :] = jnp.zeros((TAIL, SENS), BF16)
+    part_e[...] = dot(turned[...], mix_e[...]).astype(BF16)
 
 
 def sensor_kernel(turned, mix, out):
-    out[...] = dot(turned[...], mix[...]).astype(out.dtype)
+    out[...] = dot(turned[...], mix[...])
 
 
 def last_kernel(own, part_e, part_o, out):
-    total = own[...] + part_e[...].astype(F32) + part_o[...].astype(F32)
+    total = own[...] + part_e[...].astype(F32) + part_o[pl.ds(0, S), :].astype(F32)
     out[...] = total.T
 
 
@@ -466,25 +469,27 @@
         add_kernel, "add_gx_second", acc_shape, [SM, VM, VM, VM], VM, input_output_aliases={1: 0}
     )(in_smem(aims_x), on_chip(acc), gx_e, gx_o)
 
-    radiosity, part_o, turned, _ = call(
+    radiosity, part_e, part_o, turned, _ = call(
         final_kernel,
         "final_sum",
-        [pltpu.VMEM((ROWS, S), F32), pltpu.VMEM((S, SENS), BF16), pltpu.VMEM((S, ROWS), BF16), acc_shape],
-        [VM, VM, SM, VM, VM, VM, VM],
-        [VM] * 4,
-        input_output_aliases={3: 3},
-    )(emitted, rho_full, in_smem(aims_y), on_chip(acc), gy_e, gy_o, on_chip(mix_o))
-    turned = on_chip(turned)
-
-    def sensor_sums(mix, dtype, name):
-        out = call(sensor_kernel, name, pltpu.VMEM((S, SENS), dtype), [VM, VM], VM)(turned, mix)
-        return on_chip(out)
-
-    from_o = swap(part_o, "gy", 1)
-    from_e = swap(sensor_sums(on_chip(mix_e), BF16, "even_sensors"), "gy", 0)
+        [
+            pltpu.VMEM((ROWS, S), F32),
+            pltpu.VMEM((S, SENS), BF16),
+            pltpu.VMEM((S + TAIL, SENS), BF16),
+            pltpu.VMEM((S, ROWS), BF16),
+            acc_shape,
+        ],
+        [VM, VM, SM] + [VM] * 5,
+        [VM] * 5,
+        input_output_aliases={3: 4},
+    )(emitted, rho_full, in_smem(aims_y), on_chip(acc), gy_e, gy_o, on_chip(mix_e), on_chip(mix_o))
+    from_e, from_o = exchange("gy", part_e, part_o)
+    own_sum = call(sensor_kernel, "own_sensors", pltpu.VMEM((S, SENS), F32), [VM, VM], VM)(
+        on_chip(turned), mix_own
+    )
     sensor_values = call(
         last_kernel, "sensor_sum", jax.ShapeDtypeStruct((SENS, S), F32), [VM, VM, VM], VM
-    )(sensor_sums(mix_own, F32, "own_sensors"), on_chip(from_e), on_chip(from_o))
+    )(on_chip(own_sum), from_e, from_o)
     return radiosity, sensor_values
 
 

time: 58.6 us -> 58.5 us (level)
  Pallas kernels: 29.4 us -> 28.5 us
    pallas_call x2 -> x1, Pallas kernels: 1.19 us -> 0.58 us  [per_device(): call(sensor_kernel, 'own_sensors', pltpu.VMEM((S, SENS), F32), [VM, VM], VM)]
  transfers between devices with their start and end apart: 10 -> 10, of which waited for: 6 -> 4; matrix products, arithmetic and copies ran while one was open for 2% -> 2% of each run, Pallas kernels for 39% -> 37%
where the time goes in v3:
time: 58.5 us; the launch traced here: 57.6 us
  Pallas kernels  28.5 us (49%)
  starting transfers between devices  19.8 us (34%)
  waiting for transfers between devices  7.29 us (12%)
  local copies, waits for them, and re-layouts  1.16 us (2%)
  between operations  0.87 us (1%)
    ppermute x10, starting transfers between devices, swap(): lax.ppermute(x, axis, [p for a, b in pairs for p in ((a, b), (b, a))])  19.8 us
    ppermute x10, waiting for transfers between devices, swap(): lax.ppermute(x, axis, [p for a, b in pairs for p in ((a, b), (b, a))])  7.29 us
    pallas_call x1, Pallas kernels, per_device(): call(own_first_kernel, 'own_first', [acc_shape, pltpu.VMEM((ROWS, S), F32...  5.42 us
    pallas_call x1, Pallas kernels, per_device(): call(own_kernel, 'own_second', acc_shape, [SM, SM, SM, VM, VM], VM)  5.23 us
    pallas_call x1, Pallas kernels, per_device(): call(functools.partial(spread_pair_kernel, n_cols), 'spread_pair', [mix_s...  4.08 us
    pallas_call x1, Pallas kernels, per_device(): call(functools.partial(first_kernel, n_cols), 'gy_odd_terms', [pack_shape...  3.91 us
    pallas_call x1, Pallas kernels, per_device(): call(spread_own_kernel, 'spread_own', mix_shape, [VM, VM], VM)  2.03 us
    pallas_call x1, Pallas kernels, per_device(): call(functools.partial(gx_kernel, n_cols), 'gx_terms', [pack_shape(GX_ROW...  1.96 us
  transfers between devices with their start and end apart: 10, of which 4 were waited for; matrix products, arithmetic and copies ran while one was open for 2% of the time, Pallas kernels for 37%

profile of v3, /device:TPU:28, one launch (start us, length us, event | category | flops | bytes accessed | tf_op | source)
XLA Modules:
  0.0 57.6 jit_solution(17203893235564667307)
XLA Ops:
  0.6 0.0 copy-start
  0.6 3.9 %gy_odd_terms.1 = (bf16[2424,128]{1,0:T(8,128)(2,1)S(1)}, s32[128]{0:T(128)S(4)}, f32[8,512]{1,0:T(8,128)S(1)}, s32[1,144]{1,0:T(1,128)S(4)}, s32[144]{0:T(256)S...) custom-call(s32[1,144]{1,0:T(1,128)} %bitcast.9, ...), custom_call_target="tpu_custom_call" | custom-call | tf_op jit(solution)/shard_map/gy_odd_terms/pallas_call | solution.py:392
  4.6 6.4 %collective-permute-start.3 = (bf16[2424,128]{1,0:T(8,128)(2,1)S(1)}, bf16[2424,128]{1,0:T(8,128)(2,1)S(1)}, u32[]{:S(2)}, u32[]{:S(2)}) collective-permute-start(bf16[2424,128]{1,0:T(8,128)(2,1)S(1)} %get-tuple-element.44), channel_id=1, source_target_pairs={{1,2},{2,1},{3,4},{4,3},{5,6},{6,5},{7,8},{8,7},{9,10},{10,9},{11,... | collective-permute-start | bytes 1861640 | tf_op jit(solution)/shard_map/ppermute | solution.py:355
  10.9 0.0 copy-done
  11.0 0.5 gy_even_terms.1
  11.4 0.1 collective-permute-start.2
  11.5 2.0 %gx_terms.1 = (bf16[2320,128]{1,0:T(8,128)(2,1)S(1)}, bf16[2320,128]{1,0:T(8,128)(2,1)S(1)}, s32[128]{0:T(128)S(4)}, s32[256]{0:T(256)S(4)}) custom-call(s32[1,144]{1,0:T(1,128)S(4)} %get-tuple-element.31.target, s32[144]{0:T(256)S(4)} %get-tuple-element.32.source, s32[144]{0:T(256)S(4)} %get-tuple-element.33.slot, ...), custom_call_target="tpu_custom_call" | custom-call | tf_op jit(solution)/shard_map/gx_terms/pallas_call | solution.py:415
  13.5 0.0 copy-start.1
  13.5 0.1 collective-permute-start
  13.6 2.5 %collective-permute-start.1 = (bf16[2320,128]{1,0:T(8,128)(2,1)S(1)}, bf16[2320,128]{1,0:T(8,128)(2,1)S(1)}, u32[]{:S(2)}, u32[]{:S(2)}) collective-permute-start(bf16[2320,128]{1,0:T(8,128)(2,1)S(1)} %get-tuple-element.39), channel_id=1, source_target_pairs={{16,32},{32,16},{48,64},{64,48},{80,96},{96,80},{17,33},{33,17},{4... | collective-permute-start | bytes 1781768 | tf_op jit(solution)/shard_map/ppermute | solution.py:355
  16.1 2.0 %spread_own.1.mix_own.mix = bf16[3072,512]{1,0:T(8,128)(2,1)S(1)} custom-call(s32[8,512]{1,0:T(8,128)S(1)} %get-tuple-element.41.cells, f32[8,512]{1,0:T(8,128)S(1)} %get-tuple-element.42.weights), custom_call_target="tpu_custom_call" | custom-call | tf_op jit(solution)/shard_map/spread_own/pallas_call | solution.py:432
  18.2 0.0 copy-done.1
  18.2 5.4 %own_first.1 = (f32[13,256,128]{2,1,0:T(8,128)S(1)}, f32[3072,128]{1,0:T(8,128)S(1)}) custom-call(s32[256]{0:T(256)S(4)} %get-tuple-element.34.own, s32[144]{0:T(256)S(4)} %get-tuple-element.32.source, s32[144]{0:T(256)S(4)} %get-tuple-element.33.slot, bf16[144,256,256]{2,1,0:T(8,128)(2,1)S(1)} %copy-done, ...), custom_call_target="tpu_custom_call" | custom-call | tf_op jit(solution)/shard_map/own_first/pallas_call | solution.py:424
  23.6 0.0 collective-permute-done.first
  23.6 1.2 %collective-permute-done.1.second = bf16[2320,128]{1,0:T(8,128)(2,1)S(1)} collective-permute-done((bf16[2320,128]{1,0:T(8,128)(2,1)S(1)}, bf16[2320,128]{1,0:T(8,128)(2,1)S(1)}, u32[]{:S(2)}, u32[]{:S(2)}) %collective-permute-start.1) | collective-permute-done | bytes 593952 | tf_op jit(solution)/shard_map/ppermute | solution.py:355
  24.8 0.3 add_gx_first.1
  25.1 1.8 %collective-permute-done.2.gy_e = bf16[2416,128]{1,0:T(8,128)(2,1)S(1)} collective-permute-done((bf16[2416,128]{1,0:T(8,128)(2,1)S(1)}, bf16[2416,128]{1,0:T(8,128)(2,1)S(1)}, u32[]{:S(2)}, u32[]{:S(2)}) %collective-permute-start.2) | collective-permute-done | bytes 618528 | tf_op jit(solution)/shard_map/ppermute | solution.py:355
  26.9 0.0 collective-permute-done.3.gy_o
  26.9 1.0 %gy_odd_second.1 = (bf16[2320,128]{1,0:T(8,128)(2,1)S(1)}, bf16[12,256,128]{2,1,0:T(8,128)(2,1)S(1)}, s32[18]{0:T(128)S(4)}, f32[13,256,128]{2,1,0:T(8,128)S(1)}) custom-call(s32[128]{0:T(128)S(4)} %get-tuple-element.36.tab, bf16[144,256,256]{2,1,0:T(8,128)(2,1)S(1)} %copy-done, ...), custom_call_target="tpu_custom_call", output_to_operand_aliasing={{3}: (4, {})} | custom-call | tf_op jit(solution)/shard_map/gy_odd_second/pallas_call | solution.py:445
  27.9 3.8 %collective-permute-start.7 = (bf16[2320,128]{1,0:T(8,128)(2,1)S(1)}, bf16[2320,128]{1,0:T(8,128)(2,1)S(1)}, u32[]{:S(2)}, u32[]{:S(2)}) collective-permute-start(bf16[2320,128]{1,0:T(8,128)(2,1)S(1)} %get-tuple-element.51), channel_id=1, source_target_pairs={{1,2},{2,1},{3,4},{4,3},{5,6},{6,5},{7,8},{8,7},{9,10},{10,9},{11,... | collective-permute-start | bytes 1781768 | tf_op jit(solution)/shard_map/ppermute | solution.py:355
  31.7 0.5 gy_even_second.1
  32.1 0.1 collective-permute-start.6
  32.2 0.8 %gx_second.1 = (bf16[2304,128]{1,0:T(8,128)(2,1)S(1)}, bf16[2304,128]{1,0:T(8,128)(2,1)S(1)}) custom-call(s32[128]{0:T(128)S(4)} %get-tuple-element.48.tab, bf16[144,256,256]{2,1,0:T(8,128)(2,1)S(1)} %copy-done, bf16[12,256,128]{2,1,0:T(8,128)(2,1)S(1)} %get-tuple-element.47.field), custom_call_target="tpu_custom_call" | custom-call | tf_op jit(solution)/shard_map/gx_second/pallas_call | solution.py:461
  33.0 0.1 collective-permute-start.4
  33.1 2.5 %collective-permute-start.5 = (bf16[2304,128]{1,0:T(8,128)(2,1)S(1)}, bf16[2304,128]{1,0:T(8,128)(2,1)S(1)}, u32[]{:S(2)}, u32[]{:S(2)}) collective-permute-start(bf16[2304,128]{1,0:T(8,128)(2,1)S(1)} %get-tuple-element.50), channel_id=1, source_target_pairs={{16,32},{32,16},{48,64},{64,48},{80,96},{96,80},{17,33},{33,17},{4... | collective-permute-start | bytes 1769480 | tf_op jit(solution)/shard_map/ppermute | solution.py:355
  35.6 5.2 %own_second.1.acc_in = f32[13,256,128]{2,1,0:T(8,128)S(1)} custom-call(s32[256]{0:T(256)S(4)} %get-tuple-element.34.own, s32[144]{0:T(256)S(4)} %get-tuple-element.32.source, s32[144]{0:T(256)S(4)} %get-tuple-element.33.slot, bf16[144,256,256]{2,1,0:T(8,128)(2,1)S(1)} %copy-done, bf16[12,256,128]{2,1,0:T(8,128)(2,1)S(1)} %get-tuple-element.47.field), custom_call_target="tpu_custom_call" | custom-call | tf_op jit(solution)/shard_map/own_second/pallas_call | solution.py:465
  40.9 4.1 %spread_pair.1 = (bf16[3072,512]{1,0:T(8,128)(2,1)S(1)}, bf16[3072,512]{1,0:T(8,128)(2,1)S(1)}) custom-call(bf16[2416,128]{1,0:T(8,128)(2,1)S(1)} %collective-permute-done.2.gy_e, bf16[2424,128]{1,0:T(8,128)(2,1)S(1)} %collective-permute-done.3.gy_o), custom_call_target="tpu_custom_call" | custom-call | tf_op jit(solution)/shard_map/spread_pair/pallas_call | solution.py:454
  45.0 0.0 collective-permute-done.4.first
  45.0 0.0 collective-permute-done.5.second
  45.0 0.2 add_gx_second.1.acc_in
  45.2 1.0 %collective-permute-done.6.gy_e = bf16[2312,128]{1,0:T(8,128)(2,1)S(1)} collective-permute-done((bf16[2312,128]{1,0:T(8,128)(2,1)S(1)}, bf16[2312,128]{1,0:T(8,128)(2,1)S(1)}, u32[]{:S(2)}, u32[]{:S(2)}) %collective-permute-start.6) | collective-permute-done | bytes 591904 | tf_op jit(solution)/shard_map/ppermute | solution.py:355
  46.2 0.0 collective-permute-done.7.gy_o
  46.2 1.3 %final_sum.1 = (f32[3072,128]{1,0:T(8,128)S(1)}, bf16[128,512]{1,0:T(8,128)(2,1)S(1)}, bf16[136,512]{1,0:T(8,128)(2,1)S(1)}, bf16[128,3072]{1,0:T(8,128)(2,1)S(1)}, f32[13,256,128]{2,1,0:T(8,128)S(1)}) custom-call(bf16[12,256,128]{2,1,0:T(8,128)(2,1)S(1)} %get-tuple-element.30.field.emission, ...), custom_call_target="tpu_custom_call", output_to_operand_aliasing={{4}: (3, {})} | custom-call | tf_op jit(solution)/shard_map/final_sum/pallas_call | solution.py:472
  47.5 4.2 %collective-permute-start.9 = (bf16[136,512]{1,0:T(8,128)(2,1)S(1)}, bf16[136,512]{1,0:T(8,128)(2,1)S(1)}, u32[]{:S(2)}, u32[]{:S(2)}) collective-permute-start(bf16[136,512]{1,0:T(8,128)(2,1)S(1)} %get-tuple-element.57), channel_id=1, source_target_pairs={{1,2},{2,1},{3,4},{4,3},{5,6},{6,5},{7,8},{8,7},{9,10},{10,9},{11,... | collective-permute-start | bytes 417800 | tf_op jit(solution)/shard_map/ppermute | solution.py:355
  51.7 0.1 collective-permute-start.8
  51.8 0.6 %own_sensors.1.own = f32[128,512]{1,0:T(8,128)S(1)} custom-call(bf16[128,3072]{1,0:T(8,128)(2,1)S(1)} %get-tuple-element.55.turned, bf16[3072,512]{1,0:T(8,128)(2,1)S(1)} %spread_own.1.mix_own.mix), custom_call_target="tpu_custom_call" | custom-call | tf_op jit(solution)/shard_map/own_sensors/pallas_call | solution.py:487
  52.4 1.1 %copy.18 = f32[3072,128]{1,0:T(8,128)} copy(f32[3072,128]{1,0:T(8,128)S(1)} %get-tuple-element.58) | data formatting | bytes 3145728
  53.5 3.2 %collective-permute-done.8.part_e = bf16[128,512]{1,0:T(8,128)(2,1)S(1)} collective-permute-done((bf16[128,512]{1,0:T(8,128)(2,1)S(1)}, bf16[128,512]{1,0:T(8,128)(2,1)S(1)}, u32[]{:S(2)}, u32[]{:S(2)}) %collective-permute-start.8) | collective-permute-done | bytes 131104 | tf_op jit(solution)/shard_map/ppermute | solution.py:355
  56.7 0.0 collective-permute-done.9.part_o
  56.8 0.8 %sensor_sum.1 = f32[512,128]{1,0:T(8,128)} custom-call(f32[128,512]{1,0:T(8,128)S(1)} %own_sensors.1.own, bf16[128,512]{1,0:T(8,128)(2,1)S(1)} %collective-permute-done.8.part_e, bf16[136,512]{1,0:T(8,128)(2,1)S(1)} %collective-permute-done.9.part_o), custom_call_target="tpu_custom_call" | custom-call | tf_op jit(solution)/shard_map/sensor_sum/pallas_call | solution.py:490
Async XLA Ops:
  0.6 10.3 %copy-start = (bf16[144,256,256]{2,1,0:T(8,128)(2,1)S(1)}, bf16[144,256,256]{2,1,0:T(8,128)(2,1)}, u32[]{:S(2)}) copy-start(bf16[144,256,256]{2,1,0:T(8,128)(2,1)} %blocks.15) | copy-start | bytes 56623108
  4.6 22.4 %collective-permute-start.3 = (bf16[2424,128]{1,0:T(8,128)(2,1)S(1)}, bf16[2424,128]{1,0:T(8,128)(2,1)S(1)}, u32[]{:S(2)}, u32[]{:S(2)}) collective-permute-start(bf16[2424,128]{1,0:T(8,128)(2,1)S(1)} %get-tuple-element.44), channel_id=1, source_target_pairs={{1,2},{2,1},{3,4},{4,3},{5,6},{6,5},{7,8},{8,7},{9,10},{10,9},{11,... | collective-permute-start | bytes 1861640 | tf_op jit(solution)/shard_map/ppermute | solution.py:355
  11.4 15.5 %collective-permute-start.2 = (bf16[2416,128]{1,0:T(8,128)(2,1)S(1)}, bf16[2416,128]{1,0:T(8,128)(2,1)S(1)}, u32[]{:S(2)}, u32[]{:S(2)}) collective-permute-start(bf16[2416,128]{1,0:T(8,128)(2,1)S(1)} %gy_even_terms.1), channel_id=1, source_target_pairs={{0,1},{1,0},{2,3},{3,2},{4,5},{5,4},{6,7},{7,6},{8,9},{9,8},{10,11... | collective-permute-start | bytes 1855496 | tf_op jit(solution)/shard_map/ppermute | solution.py:355
  13.5 4.7 %copy-start.1 = (f32[3072]{0:T(1024)S(1)}, f32[3072]{0:T(1024)}, u32[]{:S(2)}) copy-start(f32[3072]{0:T(1024)} %param.9) | copy-start | bytes 36868
  13.5 10.1 %collective-permute-start = (bf16[2320,128]{1,0:T(8,128)(2,1)S(1)}, bf16[2320,128]{1,0:T(8,128)(2,1)S(1)}, u32[]{:S(2)}, u32[]{:S(2)}) collective-permute-start(bf16[2320,128]{1,0:T(8,128)(2,1)S(1)} %get-tuple-element.38), channel_id=1, source_target_pairs={{0,16},{16,0},{32,48},{48,32},{64,80},{80,64},{96,112},{112,96},{1... | collective-permute-start | bytes 1781768 | tf_op jit(solution)/shard_map/ppermute | solution.py:355
  13.6 11.2 %collective-permute-start.1 = (bf16[2320,128]{1,0:T(8,128)(2,1)S(1)}, bf16[2320,128]{1,0:T(8,128)(2,1)S(1)}, u32[]{:S(2)}, u32[]{:S(2)}) collective-permute-start(bf16[2320,128]{1,0:T(8,128)(2,1)S(1)} %get-tuple-element.39), channel_id=1, source_target_pairs={{16,32},{32,16},{48,64},{64,48},{80,96},{96,80},{17,33},{33,17},{4... | collective-permute-start | bytes 1781768 | tf_op jit(solution)/shard_map/ppermute | solution.py:355
  27.9 18.3 %collective-permute-start.7 = (bf16[2320,128]{1,0:T(8,128)(2,1)S(1)}, bf16[2320,128]{1,0:T(8,128)(2,1)S(1)}, u32[]{:S(2)}, u32[]{:S(2)}) collective-permute-start(bf16[2320,128]{1,0:T(8,128)(2,1)S(1)} %get-tuple-element.51), channel_id=1, source_target_pairs={{1,2},{2,1},{3,4},{4,3},{5,6},{6,5},{7,8},{8,7},{9,10},{10,9},{11,... | collective-permute-start | bytes 1781768 | tf_op jit(solution)/shard_map/ppermute | solution.py:355
  32.1 14.0 %collective-permute-start.6 = (bf16[2312,128]{1,0:T(8,128)(2,1)S(1)}, bf16[2312,128]{1,0:T(8,128)(2,1)S(1)}, u32[]{:S(2)}, u32[]{:S(2)}) collective-permute-start(bf16[2312,128]{1,0:T(8,128)(2,1)S(1)} %gy_even_second.1), channel_id=1, source_target_pairs={{0,1},{1,0},{2,3},{3,2},{4,5},{5,4},{6,7},{7,6},{8,9},{9,8},{10,11... | collective-permute-start | bytes 1775624 | tf_op jit(solution)/shard_map/ppermute | solution.py:355
  33.0 12.0 %collective-permute-start.4 = (bf16[2304,128]{1,0:T(8,128)(2,1)S(1)}, bf16[2304,128]{1,0:T(8,128)(2,1)S(1)}, u32[]{:S(2)}, u32[]{:S(2)}) collective-permute-start(bf16[2304,128]{1,0:T(8,128)(2,1)S(1)} %get-tuple-element.49), channel_id=1, source_target_pairs={{0,16},{16,0},{32,48},{48,32},{64,80},{80,64},{96,112},{112,96},{1... | collective-permute-start | bytes 1769480 | tf_op jit(solution)/shard_map/ppermute | solution.py:355
  33.1 11.9 %collective-permute-start.5 = (bf16[2304,128]{1,0:T(8,128)(2,1)S(1)}, bf16[2304,128]{1,0:T(8,128)(2,1)S(1)}, u32[]{:S(2)}, u32[]{:S(2)}) collective-permute-start(bf16[2304,128]{1,0:T(8,128)(2,1)S(1)} %get-tuple-element.50), channel_id=1, source_target_pairs={{16,32},{32,16},{48,64},{64,48},{80,96},{96,80},{17,33},{33,17},{4... | collective-permute-start | bytes 1769480 | tf_op jit(solution)/shard_map/ppermute | solution.py:355
  47.5 9.3 %collective-permute-start.9 = (bf16[136,512]{1,0:T(8,128)(2,1)S(1)}, bf16[136,512]{1,0:T(8,128)(2,1)S(1)}, u32[]{:S(2)}, u32[]{:S(2)}) collective-permute-start(bf16[136,512]{1,0:T(8,128)(2,1)S(1)} %get-tuple-element.57), channel_id=1, source_target_pairs={{1,2},{2,1},{3,4},{4,3},{5,6},{6,5},{7,8},{8,7},{9,10},{10,9},{11,... | collective-permute-start | bytes 417800 | tf_op jit(solution)/shard_map/ppermute | solution.py:355
  51.7 5.0 %collective-permute-start.8 = (bf16[128,512]{1,0:T(8,128)(2,1)S(1)}, bf16[128,512]{1,0:T(8,128)(2,1)S(1)}, u32[]{:S(2)}, u32[]{:S(2)}) collective-permute-start(bf16[128,512]{1,0:T(8,128)(2,1)S(1)} %get-tuple-element.56), channel_id=1, source_target_pairs={{0,1},{1,0},{2,3},{3,2},{4,5},{5,4},{6,7},{7,6},{8,9},{9,8},{10,11... | collective-permute-start | bytes 393224 | tf_op jit(solution)/shard_map/ppermute | solution.py:355

commit v4 on v2

--- a/solution.py
+++ b/solution.py
@@ -21,7 +21,7 @@
 META_ROWS = 3 * TAPS * SENS // S
 GX_ROWS = TERM_ROWS + SLOT_ROWS
 GY_ROWS = GX_ROWS + META_ROWS
-PAD = 16
+PAD = 8
 GROUP = 24
 OWN_SIZE = 256
 MIB = 1 << 20

time: 58.6 us -> 58.1 us (level)
  Pallas kernels: 29.4 us -> 28.8 us
  transfers between devices with their start and end apart: 10 -> 10, of which waited for: 6 -> 6; matrix products, arithmetic and copies ran while one was open for 2% -> 2% of each run, Pallas kernels for 39% -> 38%
where the time goes in v4:
time: 58.1 us; the launch traced here: 57.8 us
  Pallas kernels  28.8 us (50%)
  starting transfers between devices  19.8 us (34%)
  waiting for transfers between devices  7.24 us (12%)
  local copies, waits for them, and re-layouts  1.16 us (2%)
  between operations  0.88 us (2%)
    ppermute x10, starting transfers between devices, swap(): lax.ppermute(x, axis, [p for a, b in pairs for p in ((a, b), (b, a))])  19.8 us
    ppermute x10, waiting for transfers between devices, swap(): lax.ppermute(x, axis, [p for a, b in pairs for p in ((a, b), (b, a))])  7.24 us
    pallas_call x1, Pallas kernels, per_device(): call(own_first_kernel, 'own_first', [acc_shape, pltpu.VMEM((ROWS, S), F32...  5.62 us
    pallas_call x1, Pallas kernels, per_device(): call(own_kernel, 'own_second', acc_shape, [SM, SM, SM, VM, VM], VM)  5.05 us
    pallas_call x1, Pallas kernels, per_device(): call(functools.partial(spread_pair_kernel, n_cols), 'spread_pair', [mix_s...  4.08 us
    pallas_call x1, Pallas kernels, per_device(): call(functools.partial(first_kernel, n_cols), 'gy_odd_terms', [pack_shape...  3.91 us
    pallas_call x1, Pallas kernels, per_device(): call(spread_own_kernel, 'spread_own', mix_shape, [VM, VM], VM)  2.03 us
    pallas_call x1, Pallas kernels, per_device(): call(functools.partial(gx_kernel, n_cols), 'gx_terms', [pack_shape(GX_ROW...  1.97 us
  transfers between devices with their start and end apart: 10, of which 6 were waited for; matrix products, arithmetic and copies ran while one was open for 2% of the time, Pallas kernels for 38%

profile of v4, /device:TPU:28, one launch (start us, length us, event | category | flops | bytes accessed | tf_op | source)
XLA Modules:
  0.0 57.8 jit_solution(12277974437029525433)
XLA Ops:
  0.6 0.0 copy-start
  0.6 3.9 %gy_odd_terms.1 = (bf16[2424,128]{1,0:T(8,128)(2,1)S(1)}, s32[128]{0:T(128)S(4)}, f32[8,512]{1,0:T(8,128)S(1)}, s32[1,144]{1,0:T(1,128)S(4)}, s32[144]{0:T(256)S...) custom-call(s32[1,144]{1,0:T(1,128)} %bitcast.9, ...), custom_call_target="tpu_custom_call" | custom-call | tf_op jit(solution)/shard_map/gy_odd_terms/pallas_call | solution.py:389
  4.6 6.4 %collective-permute-start.3 = (bf16[2424,128]{1,0:T(8,128)(2,1)S(1)}, bf16[2424,128]{1,0:T(8,128)(2,1)S(1)}, u32[]{:S(2)}, u32[]{:S(2)}) collective-permute-start(bf16[2424,128]{1,0:T(8,128)(2,1)S(1)} %get-tuple-element.43), channel_id=1, source_target_pairs={{1,2},{2,1},{3,4},{4,3},{5,6},{6,5},{7,8},{8,7},{9,10},{10,9},{11,... | collective-permute-start | bytes 1861640 | tf_op jit(solution)/shard_map/ppermute | solution.py:352
  11.0 0.0 copy-done
  11.0 0.5 gy_even_terms.1
  11.4 0.1 collective-permute-start.2
  11.5 2.0 %gx_terms.1 = (bf16[2320,128]{1,0:T(8,128)(2,1)S(1)}, bf16[2320,128]{1,0:T(8,128)(2,1)S(1)}, s32[128]{0:T(128)S(4)}, s32[256]{0:T(256)S(4)}) custom-call(s32[1,144]{1,0:T(1,128)S(4)} %get-tuple-element.30.target, s32[144]{0:T(256)S(4)} %get-tuple-element.31.source, s32[144]{0:T(256)S(4)} %get-tuple-element.32.slot, ...), custom_call_target="tpu_custom_call" | custom-call | tf_op jit(solution)/shard_map/gx_terms/pallas_call | solution.py:412
  13.5 0.0 copy-start.1
  13.5 0.1 collective-permute-start
  13.6 2.5 %collective-permute-start.1 = (bf16[2320,128]{1,0:T(8,128)(2,1)S(1)}, bf16[2320,128]{1,0:T(8,128)(2,1)S(1)}, u32[]{:S(2)}, u32[]{:S(2)}) collective-permute-start(bf16[2320,128]{1,0:T(8,128)(2,1)S(1)} %get-tuple-element.38), channel_id=1, source_target_pairs={{16,32},{32,16},{48,64},{64,48},{80,96},{96,80},{17,33},{33,17},{4... | collective-permute-start | bytes 1781768 | tf_op jit(solution)/shard_map/ppermute | solution.py:352
  16.2 2.0 %spread_own.1.mix_own.mix = bf16[3072,512]{1,0:T(8,128)(2,1)S(1)} custom-call(s32[8,512]{1,0:T(8,128)S(1)} %get-tuple-element.40.cells, f32[8,512]{1,0:T(8,128)S(1)} %get-tuple-element.41.weights), custom_call_target="tpu_custom_call" | custom-call | tf_op jit(solution)/shard_map/spread_own/pallas_call | solution.py:429
  18.2 0.0 copy-done.1
  18.2 5.6 %own_first.1 = (f32[13,256,128]{2,1,0:T(8,128)S(1)}, f32[3072,128]{1,0:T(8,128)S(1)}) custom-call(s32[256]{0:T(256)S(4)} %get-tuple-element.33.own, s32[144]{0:T(256)S(4)} %get-tuple-element.31.source, s32[144]{0:T(256)S(4)} %get-tuple-element.32.slot, bf16[144,256,256]{2,1,0:T(8,128)(2,1)S(1)} %copy-done, ...), custom_call_target="tpu_custom_call" | custom-call | tf_op jit(solution)/shard_map/own_first/pallas_call | solution.py:421
  23.8 0.0 collective-permute-done.first
  23.8 1.0 %collective-permute-done.1.second = bf16[2320,128]{1,0:T(8,128)(2,1)S(1)} collective-permute-done((bf16[2320,128]{1,0:T(8,128)(2,1)S(1)}, bf16[2320,128]{1,0:T(8,128)(2,1)S(1)}, u32[]{:S(2)}, u32[]{:S(2)}) %collective-permute-start.1) | collective-permute-done | bytes 593952 | tf_op jit(solution)/shard_map/ppermute | solution.py:352
  24.9 0.3 add_gx_first.1
  25.1 1.8 %collective-permute-done.2.gy_e = bf16[2416,128]{1,0:T(8,128)(2,1)S(1)} collective-permute-done((bf16[2416,128]{1,0:T(8,128)(2,1)S(1)}, bf16[2416,128]{1,0:T(8,128)(2,1)S(1)}, u32[]{:S(2)}, u32[]{:S(2)}) %collective-permute-start.2) | collective-permute-done | bytes 618528 | tf_op jit(solution)/shard_map/ppermute | solution.py:352
  26.9 0.0 collective-permute-done.3.gy_o
  26.9 1.0 %gy_odd_second.1 = (bf16[2320,128]{1,0:T(8,128)(2,1)S(1)}, bf16[12,256,128]{2,1,0:T(8,128)(2,1)S(1)}, s32[18]{0:T(128)S(4)}, f32[13,256,128]{2,1,0:T(8,128)S(1)}) custom-call(s32[128]{0:T(128)S(4)} %get-tuple-element.35.tab, bf16[144,256,256]{2,1,0:T(8,128)(2,1)S(1)} %copy-done, ...), custom_call_target="tpu_custom_call", output_to_operand_aliasing={{3}: (4, {})} | custom-call | tf_op jit(solution)/shard_map/gy_odd_second/pallas_call | solution.py:442
  27.9 3.8 %collective-permute-start.7 = (bf16[2320,128]{1,0:T(8,128)(2,1)S(1)}, bf16[2320,128]{1,0:T(8,128)(2,1)S(1)}, u32[]{:S(2)}, u32[]{:S(2)}) collective-permute-start(bf16[2320,128]{1,0:T(8,128)(2,1)S(1)} %get-tuple-element.50), channel_id=1, source_target_pairs={{1,2},{2,1},{3,4},{4,3},{5,6},{6,5},{7,8},{8,7},{9,10},{10,9},{11,... | collective-permute-start | bytes 1781768 | tf_op jit(solution)/shard_map/ppermute | solution.py:352
  31.7 0.5 gy_even_second.1
  32.2 0.1 collective-permute-start.6
  32.2 0.8 %gx_second.1 = (bf16[2304,128]{1,0:T(8,128)(2,1)S(1)}, bf16[2304,128]{1,0:T(8,128)(2,1)S(1)}) custom-call(s32[128]{0:T(128)S(4)} %get-tuple-element.47.tab, bf16[144,256,256]{2,1,0:T(8,128)(2,1)S(1)} %copy-done, bf16[12,256,128]{2,1,0:T(8,128)(2,1)S(1)} %get-tuple-element.46.field), custom_call_target="tpu_custom_call" | custom-call | tf_op jit(solution)/shard_map/gx_second/pallas_call | solution.py:458
  33.0 0.1 collective-permute-start.4
  33.1 2.5 %collective-permute-start.5 = (bf16[2304,128]{1,0:T(8,128)(2,1)S(1)}, bf16[2304,128]{1,0:T(8,128)(2,1)S(1)}, u32[]{:S(2)}, u32[]{:S(2)}) collective-permute-start(bf16[2304,128]{1,0:T(8,128)(2,1)S(1)} %get-tuple-element.49), channel_id=1, source_target_pairs={{16,32},{32,16},{48,64},{64,48},{80,96},{96,80},{17,33},{33,17},{4... | collective-permute-start | bytes 1769480 | tf_op jit(solution)/shard_map/ppermute | solution.py:352
  35.7 5.0 %own_second.1.acc_in = f32[13,256,128]{2,1,0:T(8,128)S(1)} custom-call(s32[256]{0:T(256)S(4)} %get-tuple-element.33.own, s32[144]{0:T(256)S(4)} %get-tuple-element.31.source, s32[144]{0:T(256)S(4)} %get-tuple-element.32.slot, bf16[144,256,256]{2,1,0:T(8,128)(2,1)S(1)} %copy-done, bf16[12,256,128]{2,1,0:T(8,128)(2,1)S(1)} %get-tuple-element.46.field), custom_call_target="tpu_custom_call" | custom-call | tf_op jit(solution)/shard_map/own_second/pallas_call | solution.py:462
  40.7 4.1 %spread_pair.1 = (bf16[3072,512]{1,0:T(8,128)(2,1)S(1)}, bf16[3072,512]{1,0:T(8,128)(2,1)S(1)}) custom-call(bf16[2416,128]{1,0:T(8,128)(2,1)S(1)} %collective-permute-done.2.gy_e, bf16[2424,128]{1,0:T(8,128)(2,1)S(1)} %collective-permute-done.3.gy_o), custom_call_target="tpu_custom_call" | custom-call | tf_op jit(solution)/shard_map/spread_pair/pallas_call | solution.py:451
  44.8 0.0 collective-permute-done.4.first
  44.8 0.0 collective-permute-done.5.second
  44.8 0.2 add_gx_second.1.acc_in
  45.1 1.1 %collective-permute-done.6.gy_e = bf16[2312,128]{1,0:T(8,128)(2,1)S(1)} collective-permute-done((bf16[2312,128]{1,0:T(8,128)(2,1)S(1)}, bf16[2312,128]{1,0:T(8,128)(2,1)S(1)}, u32[]{:S(2)}, u32[]{:S(2)}) %collective-permute-start.6) | collective-permute-done | bytes 591904 | tf_op jit(solution)/shard_map/ppermute | solution.py:352
  46.2 0.1 collective-permute-done.7.gy_o
  46.3 0.9 %final_sum.1 = (f32[3072,128]{1,0:T(8,128)S(1)}, bf16[128,512]{1,0:T(8,128)(2,1)S(1)}, bf16[128,3072]{1,0:T(8,128)(2,1)S(1)}, f32[13,256,128]{2,1,0:T(8,128)S(1)}) custom-call(bf16[12,256,128]{2,1,0:T(8,128)(2,1)S(1)} %get-tuple-element.29.field.emission, f32[3072,128]{1,0:T(8,128)S(1)} %get-tuple-element.34.rho_full, ...), custom_call_target="tpu_custom_call", output_to_operand_aliasing={{3}: (3, {})} | custom-call | tf_op jit(solution)/shard_map/final_sum/pallas_call | solution.py:469
  47.2 4.2 %collective-permute-start.9 = (bf16[128,512]{1,0:T(8,128)(2,1)S(1)}, bf16[128,512]{1,0:T(8,128)(2,1)S(1)}, u32[]{:S(2)}, u32[]{:S(2)}) collective-permute-start(bf16[128,512]{1,0:T(8,128)(2,1)S(1)} %get-tuple-element.55), channel_id=1, source_target_pairs={{1,2},{2,1},{3,4},{4,3},{5,6},{6,5},{7,8},{8,7},{9,10},{10,9},{11,... | collective-permute-start | bytes 393224 | tf_op jit(solution)/shard_map/ppermute | solution.py:352
  51.4 0.6 even_sensors.1
  52.0 0.1 collective-permute-start.8
  52.1 0.6 own_sensors.1.own
  52.6 1.1 %copy.18 = f32[3072,128]{1,0:T(8,128)} copy(f32[3072,128]{1,0:T(8,128)S(1)} %get-tuple-element.56) | data formatting | bytes 3145728
  53.8 2.4 %collective-permute-done.9.part_o = bf16[128,512]{1,0:T(8,128)(2,1)S(1)} collective-permute-done((bf16[128,512]{1,0:T(8,128)(2,1)S(1)}, bf16[128,512]{1,0:T(8,128)(2,1)S(1)}, u32[]{:S(2)}, u32[]{:S(2)}) %collective-permute-start.9) | collective-permute-done | bytes 131104 | tf_op jit(solution)/shard_map/ppermute | solution.py:352
  56.2 0.9 %collective-permute-done.8.part_e = bf16[128,512]{1,0:T(8,128)(2,1)S(1)} collective-permute-done((bf16[128,512]{1,0:T(8,128)(2,1)S(1)}, bf16[128,512]{1,0:T(8,128)(2,1)S(1)}, u32[]{:S(2)}, u32[]{:S(2)}) %collective-permute-start.8) | collective-permute-done | bytes 131104 | tf_op jit(solution)/shard_map/ppermute | solution.py:352
  57.0 0.8 %sensor_sum.1 = f32[512,128]{1,0:T(8,128)} custom-call(f32[128,512]{1,0:T(8,128)S(1)} %own_sensors.1.own, bf16[128,512]{1,0:T(8,128)(2,1)S(1)} %collective-permute-done.8.part_e, bf16[128,512]{1,0:T(8,128)(2,1)S(1)} %collective-permute-done.9.part_o), custom_call_target="tpu_custom_call" | custom-call | tf_op jit(solution)/shard_map/sensor_sum/pallas_call | solution.py:485
Async XLA Ops:
  0.6 10.3 %copy-start = (bf16[144,256,256]{2,1,0:T(8,128)(2,1)S(1)}, bf16[144,256,256]{2,1,0:T(8,128)(2,1)}, u32[]{:S(2)}) copy-start(bf16[144,256,256]{2,1,0:T(8,128)(2,1)} %blocks.15) | copy-start | bytes 56623108
  4.6 22.4 %collective-permute-start.3 = (bf16[2424,128]{1,0:T(8,128)(2,1)S(1)}, bf16[2424,128]{1,0:T(8,128)(2,1)S(1)}, u32[]{:S(2)}, u32[]{:S(2)}) collective-permute-start(bf16[2424,128]{1,0:T(8,128)(2,1)S(1)} %get-tuple-element.43), channel_id=1, source_target_pairs={{1,2},{2,1},{3,4},{4,3},{5,6},{6,5},{7,8},{8,7},{9,10},{10,9},{11,... | collective-permute-start | bytes 1861640 | tf_op jit(solution)/shard_map/ppermute | solution.py:352
  11.4 15.5 %collective-permute-start.2 = (bf16[2416,128]{1,0:T(8,128)(2,1)S(1)}, bf16[2416,128]{1,0:T(8,128)(2,1)S(1)}, u32[]{:S(2)}, u32[]{:S(2)}) collective-permute-start(bf16[2416,128]{1,0:T(8,128)(2,1)S(1)} %gy_even_terms.1), channel_id=1, source_target_pairs={{0,1},{1,0},{2,3},{3,2},{4,5},{5,4},{6,7},{7,6},{8,9},{9,8},{10,11... | collective-permute-start | bytes 1855496 | tf_op jit(solution)/shard_map/ppermute | solution.py:352
  13.5 4.7 %copy-start.1 = (f32[3072]{0:T(1024)S(1)}, f32[3072]{0:T(1024)}, u32[]{:S(2)}) copy-start(f32[3072]{0:T(1024)} %param.9) | copy-start | bytes 36868
  13.5 10.3 %collective-permute-start = (bf16[2320,128]{1,0:T(8,128)(2,1)S(1)}, bf16[2320,128]{1,0:T(8,128)(2,1)S(1)}, u32[]{:S(2)}, u32[]{:S(2)}) collective-permute-start(bf16[2320,128]{1,0:T(8,128)(2,1)S(1)} %get-tuple-element.37), channel_id=1, source_target_pairs={{0,16},{16,0},{32,48},{48,32},{64,80},{80,64},{96,112},{112,96},{1... | collective-permute-start | bytes 1781768 | tf_op jit(solution)/shard_map/ppermute | solution.py:352
  13.6 11.2 %collective-permute-start.1 = (bf16[2320,128]{1,0:T(8,128)(2,1)S(1)}, bf16[2320,128]{1,0:T(8,128)(2,1)S(1)}, u32[]{:S(2)}, u32[]{:S(2)}) collective-permute-start(bf16[2320,128]{1,0:T(8,128)(2,1)S(1)} %get-tuple-element.38), channel_id=1, source_target_pairs={{16,32},{32,16},{48,64},{64,48},{80,96},{96,80},{17,33},{33,17},{4... | collective-permute-start | bytes 1781768 | tf_op jit(solution)/shard_map/ppermute | solution.py:352
  27.9 18.3 %collective-permute-start.7 = (bf16[2320,128]{1,0:T(8,128)(2,1)S(1)}, bf16[2320,128]{1,0:T(8,128)(2,1)S(1)}, u32[]{:S(2)}, u32[]{:S(2)}) collective-permute-start(bf16[2320,128]{1,0:T(8,128)(2,1)S(1)} %get-tuple-element.50), channel_id=1, source_target_pairs={{1,2},{2,1},{3,4},{4,3},{5,6},{6,5},{7,8},{8,7},{9,10},{10,9},{11,... | collective-permute-start | bytes 1781768 | tf_op jit(solution)/shard_map/ppermute | solution.py:352
  32.2 14.0 %collective-permute-start.6 = (bf16[2312,128]{1,0:T(8,128)(2,1)S(1)}, bf16[2312,128]{1,0:T(8,128)(2,1)S(1)}, u32[]{:S(2)}, u32[]{:S(2)}) collective-permute-start(bf16[2312,128]{1,0:T(8,128)(2,1)S(1)} %gy_even_second.1), channel_id=1, source_target_pairs={{0,1},{1,0},{2,3},{3,2},{4,5},{5,4},{6,7},{7,6},{8,9},{9,8},{10,11... | collective-permute-start | bytes 1775624 | tf_op jit(solution)/shard_map/ppermute | solution.py:352
  33.0 11.8 %collective-permute-start.4 = (bf16[2304,128]{1,0:T(8,128)(2,1)S(1)}, bf16[2304,128]{1,0:T(8,128)(2,1)S(1)}, u32[]{:S(2)}, u32[]{:S(2)}) collective-permute-start(bf16[2304,128]{1,0:T(8,128)(2,1)S(1)} %get-tuple-element.48), channel_id=1, source_target_pairs={{0,16},{16,0},{32,48},{48,32},{64,80},{80,64},{96,112},{112,96},{1... | collective-permute-start | bytes 1769480 | tf_op jit(solution)/shard_map/ppermute | solution.py:352
  33.1 11.7 %collective-permute-start.5 = (bf16[2304,128]{1,0:T(8,128)(2,1)S(1)}, bf16[2304,128]{1,0:T(8,128)(2,1)S(1)}, u32[]{:S(2)}, u32[]{:S(2)}) collective-permute-start(bf16[2304,128]{1,0:T(8,128)(2,1)S(1)} %get-tuple-element.49), channel_id=1, source_target_pairs={{16,32},{32,16},{48,64},{64,48},{80,96},{96,80},{17,33},{33,17},{4... | collective-permute-start | bytes 1769480 | tf_op jit(solution)/shard_map/ppermute | solution.py:352
  47.2 9.0 %collective-permute-start.9 = (bf16[128,512]{1,0:T(8,128)(2,1)S(1)}, bf16[128,512]{1,0:T(8,128)(2,1)S(1)}, u32[]{:S(2)}, u32[]{:S(2)}) collective-permute-start(bf16[128,512]{1,0:T(8,128)(2,1)S(1)} %get-tuple-element.55), channel_id=1, source_target_pairs={{1,2},{2,1},{3,4},{4,3},{5,6},{6,5},{7,8},{8,7},{9,10},{10,9},{11,... | collective-permute-start | bytes 393224 | tf_op jit(solution)/shard_map/ppermute | solution.py:352
  52.0 5.0 %collective-permute-start.8 = (bf16[128,512]{1,0:T(8,128)(2,1)S(1)}, bf16[128,512]{1,0:T(8,128)(2,1)S(1)}, u32[]{:S(2)}, u32[]{:S(2)}) collective-permute-start(bf16[128,512]{1,0:T(8,128)(2,1)S(1)} %even_sensors.1), channel_id=1, source_target_pairs={{0,1},{1,0},{2,3},{3,2},{4,5},{5,4},{6,7},{7,6},{8,9},{9,8},{10,11... | collective-permute-start | bytes 393224 | tf_op jit(solution)/shard_map/ppermute | solution.py:352
